TPU v7x, 128 devices: a whole 4x4x4 slice. The times are simulated.
128 devices in a mesh: row: 8 (over x, core), col: 16 (over y, z).
Axes of the slice: x: 4, y: 4, z: 4, core: 2. Of those that a mesh axis runs over, the one named last changes fastest.
Arguments:
- pair: float32 [1024, 1024, 128], P('row', 'col'), may hold values from -6 to 6
- logit_cotangent: bfloat16 [1024, 1024, 64], P('row', 'col'), may hold values from -6 to 6
- tiles: bfloat16 [2048, 1024, 64], P(('row', 'col')), may hold values from -6 to 6
- tile_target: int32 [2048, 1], P(('row', 'col')), may hold values from 0 to 15; in each aligned block of 16 rows (0 to 15, 16 to 31, ...) at most 2 rows name the same one
- tile_square: int32 [2048], P(('row', 'col')), may hold values from 0 to 7
- tile_count: int32 [2048], P(('row', 'col')), may hold values from 1 to 4
- w_template: bfloat16 [64, 128], replicated, may hold values from -0.75 to 0.75
- transition_norm_gain: float32 [128], replicated, may hold values from 0.1 to 1.9
- transition_norm_bias: float32 [128], replicated, may hold values from -3 to 3
- w_gate: bfloat16 [128, 512], replicated, may hold values from -0.5 to 0.5
- w_up: bfloat16 [128, 512], replicated, may hold values from -0.5 to 0.5
- w_out: bfloat16 [512, 128], replicated, may hold values from -0.25 to 0.25
- w_dist: bfloat16 [128, 64], replicated, may hold values from -0.5 to 0.5
Outputs:
- logits: bfloat16 [1024, 1024, 64], P('row', 'col')
- grad_pair: float32 [1024, 1024, 128], P('row', 'col')
- grad_tiles: bfloat16 [2048, 1024, 64], P(('row', 'col'))
- grad_template: float32 [64, 128], replicated
- grad_gain: float32 [128], replicated
- grad_bias: float32 [128], replicated
- grad_gate: float32 [128, 512], replicated
- grad_up: float32 [128, 512], replicated
- grad_out: float32 [512, 128], replicated
- grad_dist: float32 [128, 64], replicated
Inputs may be any that keep to these rules, and one draw needn't show every extreme that they name: `tile_target`: among the 16 tiles of one device no column device is named more than 2 times; some device names one exactly 2 times.
All inputs are finite; a program needn't handle non-finite values.
Results may differ from a plain program's by a relative error of at most 0.0079.
Values may be sent and summed in bfloat16 or wider, within the bound.
A program may use at most 128 MiB of HBM per device.

v0:
```python
import math

import jax
import jax.numpy as jnp
from jax import lax
from jax.sharding import PartitionSpec as P

SQ = 32
CAP = 2


def to_squares(values, across, downward):
    return (
        values.reshape(across, SQ, downward, SQ, -1)
        .transpose(0, 2, 1, 3, 4)
        .reshape(across * downward, SQ * SQ, -1)
    )


def from_squares(values, across, downward):
    return (
        values.reshape(across, downward, SQ, SQ, -1)
        .transpose(0, 2, 1, 3, 4)
        .reshape(across * SQ, downward * SQ, -1)
    )


def norm_intermediates(pair_entries, transition_norm_gain, transition_norm_bias):
    centered_entries = pair_entries - jnp.mean(pair_entries, axis=-1, keepdims=True)
    inverse_deviation = lax.rsqrt(
        jnp.mean(centered_entries * centered_entries, axis=-1, keepdims=True) + 1e-05
    )
    standardized_entries = centered_entries * inverse_deviation
    return (
        standardized_entries,
        inverse_deviation,
        (standardized_entries * transition_norm_gain + transition_norm_bias).astype(jnp.bfloat16),
    )


def transition_forward(
    pair_entries, transition_norm_gain, transition_norm_bias, w_gate, w_up, w_out
):
    standardized_entries, inverse_deviation, normalized_entries = norm_intermediates(
        pair_entries, transition_norm_gain, transition_norm_bias
    )
    gate = jnp.dot(normalized_entries, w_gate, preferred_element_type=jnp.float32)
    upper = jnp.dot(normalized_entries, w_up, preferred_element_type=jnp.float32)
    hidden = (jax.nn.silu(gate) * upper).astype(jnp.bfloat16)
    return pair_entries + jnp.dot(hidden, w_out, preferred_element_type=jnp.float32)


def transition_backward(
    pair_entries, upstream, transition_norm_gain, transition_norm_bias, w_gate, w_up, w_out
):
    standardized_entries, inverse_deviation, normalized_entries = norm_intermediates(
        pair_entries, transition_norm_gain, transition_norm_bias
    )
    gate = jnp.dot(normalized_entries, w_gate, preferred_element_type=jnp.float32)
    upper = jnp.dot(normalized_entries, w_up, preferred_element_type=jnp.float32)
    sigma = jax.nn.sigmoid(gate)
    swish = gate * sigma
    hidden = (swish * upper).astype(jnp.bfloat16)
    up_low = upstream.astype(jnp.bfloat16)
    g_out = jnp.dot(hidden.T, up_low, preferred_element_type=jnp.float32)
    d_hidden = jnp.dot(up_low, w_out.T, preferred_element_type=jnp.float32)
    d_gate = (d_hidden * upper * sigma * (1.0 + gate * (1.0 - sigma))).astype(jnp.bfloat16)
    d_upper = (d_hidden * swish).astype(jnp.bfloat16)
    g_gate = jnp.dot(normalized_entries.T, d_gate, preferred_element_type=jnp.float32)
    g_up = jnp.dot(normalized_entries.T, d_upper, preferred_element_type=jnp.float32)
    normalized_gradient = jnp.dot(d_gate, w_gate.T, preferred_element_type=jnp.float32) + jnp.dot(
        d_upper, w_up.T, preferred_element_type=jnp.float32
    )
    gain_gradient = jnp.sum(normalized_gradient * standardized_entries, axis=0)
    g_bias = jnp.sum(normalized_gradient, axis=0)
    standardized_gradient = normalized_gradient * transition_norm_gain
    entries_gradient = (
        standardized_gradient
        - jnp.mean(standardized_gradient, axis=-1, keepdims=True)
        - standardized_entries
        * jnp.mean(standardized_gradient * standardized_entries, axis=-1, keepdims=True)
    ) * inverse_deviation
    return (upstream + entries_gradient, (gain_gradient, g_bias, g_gate, g_up, g_out))


def mirror(block, row_devs, col_devs):
    rows_here, cols_here, bins = block.shape
    piece = rows_here // col_devs
    devices = row_devs * col_devs
    spread = lax.all_to_all(block, "col", split_axis=0, concat_axis=1, tiled=True)
    split = spread.reshape(piece, devices, piece, bins)
    moved = lax.all_to_all(split, ("row", "col"), split_axis=1, concat_axis=0, tiled=True)
    columns = moved.reshape(devices * piece, piece, bins)
    flipped = columns.transpose(1, 0, 2)
    return lax.all_to_all(flipped, "col", split_axis=1, concat_axis=0, tiled=True)


def per_device(
    pair,
    logit_cotangent,
    tiles,
    tile_target,
    tile_square,
    tile_count,
    w_template,
    transition_norm_gain,
    transition_norm_bias,
    w_gate,
    w_up,
    w_out,
    w_dist,
):
    row_devs = lax.axis_size("row")
    col_devs = lax.axis_size("col")
    rows_here, cols_here, width = pair.shape
    bins = w_dist.shape[1]
    length = rows_here * row_devs
    slots, cells_sq, feature = tiles.shape
    sq_rows = rows_here // SQ
    sq_cols = cols_here // SQ
    squares = sq_rows * sq_cols
    mirrored_cot = mirror(logit_cotangent, row_devs, col_devs)
    target = tile_target[:, 0]
    positions = jnp.arange(slots, dtype=jnp.int32)
    earlier = positions[None, :] < positions[:, None]
    same_target = target[:, None] == target[None, :]
    slot_rank = jnp.sum((same_target & earlier).astype(jnp.int32), axis=1)
    chooser_bool = (
        target[:, None, None] == jnp.arange(col_devs, dtype=jnp.int32)[None, :, None]
    ) & (slot_rank[:, None, None] == jnp.arange(CAP, dtype=jnp.int32)[None, None, :])
    chooser_int = chooser_bool.astype(jnp.int32)
    chooser = chooser_bool.astype(jnp.bfloat16)
    occupied = jnp.sum(chooser_int, axis=0)
    send_ids = jnp.sum(chooser_int * (tile_square + 1)[:, None, None], axis=0) - 1
    send_counts = jnp.sum(chooser_int * tile_count[:, None, None], axis=0) + 1 - occupied
    counts_f = tile_count.astype(jnp.float32)
    proj = jnp.dot(
        tiles.reshape(slots * cells_sq, feature), w_template, preferred_element_type=jnp.float32
    )
    proj = (proj.reshape(slots, cells_sq, width) / counts_f[:, None, None]).astype(jnp.bfloat16)
    payload = jnp.einsum("sdk,spc->dkpc", chooser, proj, preferred_element_type=jnp.float32).astype(
        jnp.bfloat16
    )
    received, got_ids, got_counts = (
        lax.all_to_all(payload, "col", split_axis=0, concat_axis=0, tiled=True),
        lax.all_to_all(send_ids, "col", split_axis=0, concat_axis=0, tiled=True),
        lax.all_to_all(send_counts, "col", split_axis=0, concat_axis=0, tiled=True),
    )
    incoming = col_devs * CAP
    got_ids = got_ids.reshape(incoming)
    proj_in = received.reshape(incoming, cells_sq, width)
    placing = (got_ids[:, None] == jnp.arange(squares, dtype=jnp.int32)[None, :]).astype(
        jnp.bfloat16
    )
    added = jnp.einsum("ns,npc->spc", placing, proj_in, preferred_element_type=jnp.float32)
    z_one = pair + from_squares(added, sq_rows, sq_cols)
    pair_entries = rows_here * cols_here
    block = math.gcd(pair_entries, 2048)
    blocks = pair_entries // block
    z_blocks = z_one.reshape(blocks, block, width)
    z_two = lax.map(
        lambda piece: transition_forward(
            piece, transition_norm_gain, transition_norm_bias, w_gate, w_up, w_out
        ),
        z_blocks,
    )
    z_low = z_two.reshape(pair_entries, width).astype(jnp.bfloat16)
    heads = (
        jnp.dot(z_low, w_dist, preferred_element_type=jnp.float32)
        .astype(jnp.bfloat16)
        .reshape(rows_here, cols_here, bins)
    )
    heads_mirror = mirror(heads, row_devs, col_devs)
    logits = (heads.astype(jnp.float32) + heads_mirror.astype(jnp.float32)).astype(jnp.bfloat16)
    d_heads = (
        (logit_cotangent.astype(jnp.float32) + mirrored_cot.astype(jnp.float32))
        .astype(jnp.bfloat16)
        .reshape(pair_entries, bins)
    )
    dz_two = jnp.dot(d_heads, w_dist.T, preferred_element_type=jnp.float32)
    g_dist = jnp.dot(z_low.T, d_heads, preferred_element_type=jnp.float32)

    def back_block(carry, items):
        piece, upstream = items
        d_piece, grads = transition_backward(
            piece, upstream, transition_norm_gain, transition_norm_bias, w_gate, w_up, w_out
        )
        return (tuple((total + term for total, term in zip(carry, grads))), d_piece)

    hidden_units = w_gate.shape[1]
    start = (
        jnp.zeros((width,), jnp.float32),
        jnp.zeros((width,), jnp.float32),
        jnp.zeros((width, hidden_units), jnp.float32),
        jnp.zeros((width, hidden_units), jnp.float32),
        jnp.zeros((hidden_units, width), jnp.float32),
    )
    sums, dz_one = lax.scan(back_block, start, (z_blocks, dz_two.reshape(blocks, block, width)))
    grad_pair = dz_one.reshape(rows_here, cols_here, width)
    d_squares = to_squares(grad_pair, sq_rows, sq_cols)
    valid = (got_ids >= 0).astype(jnp.float32)
    picked = jnp.take(d_squares, jnp.maximum(got_ids, 0), axis=0)
    d_proj_in = (picked * valid[:, None, None]).astype(jnp.bfloat16)
    returned = lax.all_to_all(
        d_proj_in.reshape(col_devs, CAP, cells_sq, width),
        "col",
        split_axis=0,
        concat_axis=0,
        tiled=True,
    )
    d_proj = jnp.einsum(
        "sdk,dkpc->spc", chooser, returned, preferred_element_type=jnp.float32
    ).astype(jnp.bfloat16)
    g_tile = jnp.dot(
        d_proj.reshape(slots * cells_sq, width), w_template.T, preferred_element_type=jnp.float32
    )
    grad_tiles = (g_tile.reshape(slots, cells_sq, feature) / counts_f[:, None, None]).astype(
        jnp.bfloat16
    )
    per_slot = jnp.einsum("spt,spc->stc", tiles, d_proj, preferred_element_type=jnp.float32)
    g_template = jnp.sum(per_slot / counts_f[:, None, None], axis=0)
    totals = lax.psum(
        (g_template, sums[0], sums[1], sums[2], sums[3], sums[4], g_dist), ("row", "col")
    )
    scale = jnp.float32(length)
    return (
        logits,
        grad_pair,
        grad_tiles,
        totals[0] / scale,
        totals[1] / scale,
        totals[2] / scale,
        totals[3] / scale,
        totals[4] / scale,
        totals[5] / scale,
        totals[6] / scale,
    )


def solution(mesh):
    return jax.shard_map(
        per_device,
        mesh=mesh,
        in_specs=(
            P("row", "col", None),
            P("row", "col", None),
            P(("row", "col"), None, None),
            P(("row", "col"), None),
            P(("row", "col")),
            P(("row", "col")),
            P(),
            P(),
            P(),
            P(),
            P(),
            P(),
            P(),
        ),
        out_specs=(
            P("row", "col", None),
            P("row", "col", None),
            P(("row", "col"), None, None),
            P(),
            P(),
            P(),
            P(),
            P(),
            P(),
            P(),
        ),
        check_vma=False,
    )
```

profile of v0, /device:TPU:1, one launch (start us, length us, event | category | flops | bytes accessed | tf_op | source)
XLA Modules:
  0.0 950.0 jit_solution(895207414862114113)
XLA Ops:
  13.4 8.6 all-to-all-start.5
  23.2 6.2 copy.143
  29.3 8.4 all-to-all-done.5
  48.0 9.8 %all-to-all-start.6 = ((bf16[128,2,2048]{2,1,0:T(2,128)(2,1)}), bf16[128,2,2048]{2,1,0:T(2,128)(2,1)S(1)}, u32[]{:S(2)}, u32[]{:S(2)}) async-start(bf16[128,2,2048]{2,1,0:T(2,128)(2,1)} %reshape.291), calls=%async_computation.6 | async-start | bytes 2097152 | tf_op jit(solution)/shard_map/all_to_all | solution.py:92
  57.8 8.1 convolution_convert_fusion.1
  65.9 8.8 copy.145
  95.0 136.2 %all-to-all-done.1 = bf16[16,2,1024,128]{3,2,1,0:T(8,128)(2,1)} async-done(((bf16[16,2,1024,128]{3,2,1,0:T(8,128)(2,1)}), bf16[16,2,1024,128]{3,2,1,0:T(8,128)(2,1)}, u32[]{:S(2)}, u32[]{:S(2)}) %all-to-all-start.1) | async-done | bytes 8388640 | tf_op jit(solution)/shard_map/all_to_all | solution.py:145
  231.2 9.6 %all-to-all-start.7 = ((bf16[16,2,16384]{2,1,0:T(2,128)(2,1)}), bf16[16,2,16384]{2,1,0:T(2,128)(2,1)}, u32[]{:S(2)}, u32[]{:S(2)}) async-start(bf16[16,2,16384]{2,1,0:T(2,128)(2,1)} %reshape.293), calls=%async_computation.7 | async-start | bytes 2097152 | tf_op jit(solution)/shard_map/all_to_all | solution.py:95
  240.8 12.0 %copy.146 = bf16[1024,128,32]{1,2,0:T(8,128)(2,1)} copy(bf16[1024,128,32]{1,0,2:T(8,128)(2,1)} %bitcast.10) | data formatting | bytes 16777216 | tf_op jit(solution)/shard_map/ns,npc->spc/dot_general | solution.py:155
  262.6 48.9 %while.33 = (s32[]{:T(128)}, bf16[4,2048,128]{2,1,0:T(8,128)(2,1)S(1)}, f32[4,2048,128]{2,1,0:T(8,128)}, f32[128]{0:T(128)S(1)}, f32[128]{0:T(128)S(1)}, /*index...) while((s32[]{:T(128)}, ...), condition=%wide.region_5.6_spmd.clone, body=%wide.region_2.5_spmd.sunk.clone | while | flops 815532032 | bytes 15166569 | solution.py:161
  326.6 6.7 all-to-all-start.2
  344.4 5.7 copy.158
  376.3 12.3 %all-to-all-start.3 = ((bf16[128,2,2048]{2,1,0:T(2,128)(2,1)}), bf16[128,2,2048]{2,1,0:T(2,128)(2,1)}, u32[]{:S(2)}, u32[]{:S(2)}) async-start(bf16[128,2,2048]{2,1,0:T(2,128)(2,1)} %reshape.285), calls=%async_computation.3 | async-start | bytes 2097152 | tf_op jit(solution)/shard_map/all_to_all | solution.py:92
  388.6 68.5 %while.34 = (s32[]{:T(128)}, f32[128]{0:T(128)S(1)}, f32[128]{0:T(128)S(1)}, f32[128,512]{1,0:T(8,128)S(1)}, f32[128,512]{1,0:T(8,128)S(1)}, /*index=5*/f32[512,...) while((s32[]{:T(128)}, f32[128]{0:T(128)S(1)}, ...), condition=%wide.region_13.14_spmd.clone.clone, body=%wide.region_6.13_spmd.clone.sunk.clone | while | flops 2174880000 | bytes 88914152 | solution.py:198
  462.2 10.1 %gather_fusion = f32[32,1024,128]{2,1,0:T(8,128)} fusion(f32[8,1024,128]{2,1,0:T(8,128)} %bitcast.257, s32[1024]{0:T(1024)S(1)} %pad_clamp_fusion), kind=kCustom, calls=%fused_computation | custom fusion | bytes 33554560 | tf_op jit(solution)/shard_map/jit(_take)/gather | solution.py:202
  478.4 7.9 all-to-all-start.4
  486.3 6.9 multiply_convert_fusion.7
  493.3 7.7 copy.168
  503.0 5.9 all-to-all-start.8
  514.1 242.8 %all-reduce.7.cloned.1.call-done = (f32[128,512]{1,0:T(8,128)}, f32[128,512]{1,0:T(8,128)}, f32[512,128]{1,0:T(8,128)}) async-done(((f32[128,512]{1,0:T(8,128)}, f32[128,512]{1,0:T(8,128)}, f32[512,128]{1,0:T(8,128)}), (f32[128,512]{1,0:T(8,128)}, f32[128,512]{1,0:T(8,128)}, f32[512,128]{1,0:T(8,128)})) %all-reduce.7.cloned.1.call-update) | async-done | bytes 786448 | tf_op jit(solution)/shard_map/psum | solution.py:222
  774.0 5.8 copy.153
  787.6 8.6 bitcast_convert_fusion.3
  799.4 6.1 divide_convert_fusion.1
  805.5 133.5 %all-reduce.5.cloned.1.call-done = (f32[64,128]{1,0:T(8,128)}, f32[128]{0:T(128)}, f32[128]{0:T(128)}, f32[128,64]{0,1:T(8,128)}) async-done(((f32[64,128]{1,0:T(8,128)}, f32[128]{0:T(128)}, f32[128]{0:T(128)}, f32[128,64]{0,1:T(8,128)}), (f32[64,128]{1,0:T(8,128)}, f32[128]{0:T(128)}, f32[128]{0:T(128)}, f32[128,64]{0,1:T(8,128)})) %all-reduce.5.cloned.1.call-update) | async-done | bytes 66576 | tf_op jit(solution)/shard_map/psum | solution.py:222
  (252 shorter events, 266.6 us)
Async XLA Ops:
  7.2 50.6 %copy-start = (bf16[64,128]{1,0:T(8,128)(2,1)S(1)}, bf16[64,128]{1,0:T(8,128)(2,1)}, u32[]{:S(2)}) copy-start(bf16[64,128]{1,0:T(8,128)(2,1)} %param.23) | copy-start | bytes 49156
  7.2 14.8 %copy-start.30 = (s32[16]{0:T(128)S(1)}, s32[16]{0:T(128)}, u32[]{:S(2)}) copy-start(s32[16]{0:T(128)} %param.22) | copy-start | bytes 196
  7.2 14.9 %copy-start.28 = (s32[16,1]{0,1:T(1,128)S(1)}, s32[16,1]{0,1:T(1,128)}, u32[]{:S(2)}) copy-start(s32[16,1]{0,1:T(1,128)} %param.20) | copy-start | bytes 196
  7.2 15.1 %copy-start.31 = (s32[16]{0:T(128)S(1)}, s32[16]{0:T(128)}, u32[]{:S(2)}) copy-start(s32[16]{0:T(128)} %param.21) | copy-start | bytes 196
  13.4 24.3 %all-to-all-start.5 = ((bf16[16,2,16384]{2,1,0:T(2,128)(2,1)}), bf16[16,2,16384]{2,1,0:T(2,128)(2,1)S(1)}, u32[]{:S(2)}, u32[]{:S(2)}) async-start(bf16[16,2,16384]{2,1,0:T(2,128)(2,1)} %reshape.289), calls=%async_computation.5 | async-start | bytes 2097152 | tf_op jit(solution)/shard_map/all_to_all | solution.py:90
  22.1 35.7 %copy-start.32 = (f32[16]{0:T(128)}, f32[16]{0:T(128)S(1)}, u32[]{:S(2)}) copy-start(f32[16]{0:T(128)S(1)} %convert_element_type.103) | copy-start | bytes 196
  22.3 35.5 %copy-start.26 = (pred[16,2]{0,1:T(4,128)(4,1)}, pred[16,2]{0,1:T(4,128)(4,1)S(1)}, u32[]{:S(2)}) copy-start(pred[16,2]{0,1:T(4,128)(4,1)S(1)} %iota_compare_fusion.2) | copy-start | bytes 100
  22.4 35.4 %copy-start.23 = (pred[16,16]{1,0:T(8,128)(4,1)}, pred[16,16]{1,0:T(8,128)(4,1)S(1)}, u32[]{:S(2)}) copy-start(pred[16,16]{1,0:T(8,128)(4,1)S(1)} %iota_compare_fusion.1) | copy-start | bytes 772
  37.7 10.3 %all-to-all-start = ((s32[16,1,2]{2,1,0:T(1,128)}), s32[16,1,2]{2,1,0:T(1,128)S(1)}, u32[]{:S(2)}, u32[]{:S(2)}) async-start(s32[16,1,2]{2,1,0:T(1,128)} %copy.142), calls=%async_computation | async-start | bytes 16384 | tf_op jit(solution)/shard_map/all_to_all | solution.py:146
  48.0 28.8 %all-to-all-start.6 = ((bf16[128,2,2048]{2,1,0:T(2,128)(2,1)}), bf16[128,2,2048]{2,1,0:T(2,128)(2,1)S(1)}, u32[]{:S(2)}, u32[]{:S(2)}) async-start(bf16[128,2,2048]{2,1,0:T(2,128)(2,1)} %reshape.291), calls=%async_computation.6 | async-start | bytes 2097152 | tf_op jit(solution)/shard_map/all_to_all | solution.py:92
  77.7 153.5 %all-to-all-start.1 = ((bf16[16,2,1024,128]{3,2,1,0:T(8,128)(2,1)}), bf16[16,2,1024,128]{3,2,1,0:T(8,128)(2,1)}, u32[]{:S(2)}, u32[]{:S(2)}) async-start(bf16[16,2,1024,128]{3,2,1,0:T(8,128)(2,1)} %copy.145), calls=%async_computation.1 | async-start | bytes 16777216 | tf_op jit(solution)/shard_map/all_to_all | solution.py:145
  231.2 95.4 %all-to-all-start.7 = ((bf16[16,2,16384]{2,1,0:T(2,128)(2,1)}), bf16[16,2,16384]{2,1,0:T(2,128)(2,1)}, u32[]{:S(2)}, u32[]{:S(2)}) async-start(bf16[16,2,16384]{2,1,0:T(2,128)(2,1)} %reshape.293), calls=%async_computation.7 | async-start | bytes 2097152 | tf_op jit(solution)/shard_map/all_to_all | solution.py:95
  262.6 49.0 %copy-start.18 = (bf16[128,64]{0,1:T(8,128)(2,1)S(1)}, bf16[128,64]{0,1:T(8,128)(2,1)}, u32[]{:S(2)}) copy-start(bf16[128,64]{0,1:T(8,128)(2,1)} %param.29) | copy-start | bytes 49156
  326.6 38.7 %all-to-all-start.2 = ((bf16[16,2,16384]{2,1,0:T(2,128)(2,1)}), bf16[16,2,16384]{2,1,0:T(2,128)(2,1)}, u32[]{:S(2)}, u32[]{:S(2)}) async-start(bf16[16,2,16384]{2,1,0:T(2,128)(2,1)} %reshape.283), calls=%async_computation.2 | async-start | bytes 2097152 | tf_op jit(solution)/shard_map/all_to_all | solution.py:90
  376.3 96.1 %all-to-all-start.3 = ((bf16[128,2,2048]{2,1,0:T(2,128)(2,1)}), bf16[128,2,2048]{2,1,0:T(2,128)(2,1)}, u32[]{:S(2)}, u32[]{:S(2)}) async-start(bf16[128,2,2048]{2,1,0:T(2,128)(2,1)} %reshape.285), calls=%async_computation.3 | async-start | bytes 2097152 | tf_op jit(solution)/shard_map/all_to_all | solution.py:92
  472.4 13.9 %copy-start.20 = (f32[16,2]{1,0:T(8,128)S(1)}, f32[16,2]{1,0:T(8,128)}, u32[]{:S(2)}) copy-start(f32[16,2]{1,0:T(8,128)} %copy.167) | copy-start | bytes 388
  472.4 13.9 %copy-start.25 = (pred[16,2]{1,0:T(8,128)(4,1)S(1)}, pred[16,2]{1,0:T(8,128)(4,1)}, u32[]{:S(2)}) copy-start(pred[16,2]{1,0:T(8,128)(4,1)} %copy.163) | copy-start | bytes 100
  478.4 23.5 %all-to-all-start.4 = ((bf16[16,2,16384]{2,1,0:T(2,128)(2,1)}), bf16[16,2,16384]{2,1,0:T(2,128)(2,1)S(1)}, u32[]{:S(2)}, u32[]{:S(2)}) async-start(bf16[16,2,16384]{2,1,0:T(2,128)(2,1)} %reshape.287), calls=%async_computation.4 | async-start | bytes 2097152 | tf_op jit(solution)/shard_map/all_to_all | solution.py:95
  501.0 12.0 %copy-start.3 = (bf16[4,2048,128]{2,1,0:T(8,128)(2,1)S(1)}, bf16[4,2048,128]{2,1,0:T(8,128)(2,1)}, u32[]{:S(2)}) copy-start(bf16[4,2048,128]{2,1,0:T(8,128)(2,1)} %copy-done.2) | copy-start | bytes 6291460
  503.0 284.6 %all-to-all-start.8 = ((bf16[16,2,1024,128]{3,1,2,0:T(2,128)(2,1)}), bf16[16,2,1024,128]{3,1,2,0:T(2,128)(2,1)}, u32[]{:S(2)}, u32[]{:S(2)}) async-start(bf16[16,2,1024,128]{3,1,2,0:T(2,128)(2,1)} %copy.168), calls=%async_computation.8 | async-start | bytes 16777216 | tf_op jit(solution)/shard_map/all_to_all | solution.py:204
  508.9 248.1 %all-reduce.7.cloned.1.call-start = ((), (), s32[]{:S(2)}) async-start(), calls=%async_computation.10 | async-start | bytes 1572864 | tf_op jit(solution)/shard_map/psum | solution.py:222
  509.6 429.4 %all-reduce.5.cloned.1.call-start = ((), (), s32[]{:S(2)}) async-start(), calls=%async_computation.9 | async-start | bytes 133120 | tf_op jit(solution)/shard_map/psum | solution.py:222
  787.6 8.7 copy-start.15
  787.6 8.7 copy-start.33
  (27 other events, 98.5 us)
Sparse Core Ops, SparseCore 0:
  515.9 241.0 all-reduce.6
  799.5 139.4 all-reduce.4
where the time goes:
time: 961 us; the launch traced here: 950 us
  waiting for transfers between devices  527 us (55%)
  local copies, waits for them, and re-layouts  163 us (17%)
  matrix products  104 us (11%)
  starting transfers between devices  70.4 us (7%)
  other arithmetic  70.3 us (7%)
  between operations  14.9 us (2%)
    psum x2, waiting for transfers between devices, per_device(): lax.psum((g_template, sums[0], sums[1], sums[2], sums[3], sums[4], g_dist...  376 us
    all_to_all x1, waiting for transfers between devices, per_device(): lax.all_to_all(payload, 'col', split_axis=0, concat_axis=0, tiled=True)  136 us
    unnamed x79, local copies, waits for them, and re-layouts  56.9 us
    all_to_all x2, starting transfers between devices, mirror(): lax.all_to_all(split, ('row', 'col'), split_axis=1, concat_axis=0, tiled=...  22.1 us
  transfers between devices with their start and end apart: 11, of which 7 were waited for; matrix products, arithmetic and copies ran while one was open for 31% of the time, Pallas kernels for 0%

commit v1 on v0

v1 whole, which is shorter than its diff:
```python
import functools

import jax
import jax.numpy as jnp
from jax import lax
from jax.experimental import pallas as pl
from jax.experimental.pallas import tpu as pltpu
from jax.sharding import PartitionSpec as P

SQ = 32
CAP = 2
MESH = pl.DeviceIdType.MESH
F32 = jnp.float32
BF16 = jnp.bfloat16
ROWS_SUM = 2048
VMEM_LIMIT = 60 * 1024 * 1024


def vmem():
    return pl.BlockSpec(memory_space=pltpu.VMEM)


def smem():
    return pl.BlockSpec(memory_space=pltpu.SMEM)


def hbm():
    return pl.BlockSpec(memory_space=pl.ANY)


def nn(a, b):
    return lax.dot_general(a, b, (((1,), (0,)), ((), ())), preferred_element_type=F32)


def nt(a, b):
    return lax.dot_general(a, b, (((1,), (1,)), ((), ())), preferred_element_type=F32)


def tn(a, b):
    return lax.dot_general(a, b, (((0,), (0,)), ((), ())), preferred_element_type=F32)


def displacements(col_devs):
    if col_devs != 16:
        return (1, col_devs), [(0, k) for k in range(1, col_devs)]
    order = [(0, 1), (1, 0), (0, 3), (3, 0), (1, 1), (3, 3), (1, 3), (3, 1),
             (0, 2), (2, 0), (1, 2), (2, 1), (3, 2), (2, 3), (2, 2)]
    return (4, 4), order


def moved(col, shape, step, sign):
    ys, zs = shape
    y = lax.rem(col // zs + sign * step[0] + ys, ys)
    z = lax.rem(lax.rem(col, zs) + sign * step[1] + zs, zs)
    return y * zs + z


def mirror_copies(row, col, src, dst, send_sem, recv_sem):
    out = []
    for h in (0, 1):
        to_row, to_col = col // 2, 2 * row + h
        here = jnp.logical_and(to_row == row, to_col == col)
        slot = lax.rem(col, 2)
        remote = pltpu.make_async_remote_copy(
            src_ref=src[h], dst_ref=dst.at[slot], send_sem=send_sem.at[h],
            recv_sem=recv_sem.at[slot], device_id=(to_row, to_col), device_id_type=MESH)
        local = pltpu.make_async_copy(src[h], dst.at[slot], recv_sem.at[slot])
        out.append((here, remote, local))
    return out


def start_mirror(copies):
    for here, remote, local in copies:
        @pl.when(jnp.logical_not(here))
        def _():
            remote.start()

        @pl.when(here)
        def _():
            local.start()


def wait_mirror(copies, src, dst, recv_sem):
    for h, (here, remote, local) in enumerate(copies):
        @pl.when(jnp.logical_not(here))
        def _():
            remote.wait_send()

        pltpu.make_async_copy(src[h], dst.at[h], recv_sem.at[h]).wait()


def greet(row, col, row_devs, col_devs, rows_too):
    barrier = pltpu.get_barrier_semaphore()
    shape, order = displacements(col_devs)
    for step in order:
        pl.semaphore_signal(barrier, inc=1, device_id=(row, moved(col, shape, step, 1)), device_id_type=MESH)
    count = len(order)
    if rows_too:
        for k in range(1, row_devs):
            pl.semaphore_signal(
                barrier, inc=1, device_id=(lax.rem(row + k, row_devs), col), device_id_type=MESH)
        count += row_devs - 1
    for h in (0, 1):
        to_row, to_col = col // 2, 2 * row + h

        @pl.when(jnp.logical_not(jnp.logical_and(to_row == row, to_col == col)))
        def _():
            pl.semaphore_signal(barrier, inc=1, device_id=(to_row, to_col), device_id_type=MESH)
    return barrier, count


def greeted(row, col, barrier, count):
    here = (col // 2 == row).astype(jnp.int32)
    pl.semaphore_wait(barrier, count + 2 - here)


def exchange_kernel(row_devs, col_devs, idx_ref, inv_ref, ids_ref, tiles_ref, cot_ref,
                    recv_ref, got_ref, mir_ref, sendbuf, pack, dma_send, dma_recv, id_send, id_recv,
                    own_sem, mir_send, mir_recv):
    row, col = lax.axis_index("row"), lax.axis_index("col")
    shape, order = displacements(col_devs)
    barrier, count = greet(row, col, row_devs, col_devs, False)

    bins, lanes = cot_ref.shape[1:]
    low = lax.broadcasted_iota(jnp.int32, (bins, lanes), 1) < lanes // 2

    def pack_pair(k, carry):
        a, b = cot_ref[2 * k].astype(F32), cot_ref[2 * k + 1].astype(F32)
        pack[0, k] = jnp.where(low, a, pltpu.roll(b, lanes // 2, 1)).astype(BF16)
        pack[1, k] = jnp.where(low, pltpu.roll(a, lanes // 2, 1), b).astype(BF16)
        return carry

    lax.fori_loop(0, cot_ref.shape[0] // 2, pack_pair, 0)

    def fill(d, carry):
        for k in range(CAP):
            sendbuf[d, k] = (tiles_ref[idx_ref[d, k]].astype(F32) * inv_ref[d, k]).astype(BF16)
        return carry

    lax.fori_loop(0, col_devs, fill, 0)
    greeted(row, col, barrier, count)

    mirror = mirror_copies(row, col, (pack.at[0], pack.at[1]), mir_ref, mir_send, mir_recv)
    start_mirror(mirror)
    copies = []
    for k, step in enumerate(order):
        to = moved(col, shape, step, 1)
        copies.append(pltpu.make_async_remote_copy(
            src_ref=sendbuf.at[to], dst_ref=recv_ref.at[col], send_sem=dma_send.at[k],
            recv_sem=dma_recv.at[k], device_id=(row, to), device_id_type=MESH))
        copies.append(pltpu.make_async_remote_copy(
            src_ref=ids_ref.at[to], dst_ref=got_ref.at[col], send_sem=id_send.at[k],
            recv_sem=id_recv.at[k], device_id=(row, to), device_id_type=MESH))
    for copy in copies:
        copy.start()
    own = pltpu.make_async_copy(sendbuf.at[col], recv_ref.at[col], own_sem.at[0])
    own_id = pltpu.make_async_copy(ids_ref.at[col], got_ref.at[col], own_sem.at[1])
    own.start()
    own_id.start()
    own.wait()
    own_id.wait()
    for copy in copies:
        copy.wait()
    wait_mirror(mirror, (pack.at[0], pack.at[1]), mir_ref, mir_recv)


def exchange(row_devs, col_devs, idx, inv, ids, tiles_t, cot_t):
    slots, feature, cells = tiles_t.shape
    cols, bins, rows = cot_t.shape
    peers = col_devs - 1
    return pl.pallas_call(
        functools.partial(exchange_kernel, row_devs, col_devs),
        name="exchange",
        out_shape=(
            jax.ShapeDtypeStruct((col_devs, CAP, feature, cells), BF16),
            jax.ShapeDtypeStruct((col_devs, 8, 128), jnp.int32),
            jax.ShapeDtypeStruct((2, cols // 2, bins, rows), BF16),
        ),
        in_specs=[smem(), smem(), vmem(), vmem(), vmem()],
        out_specs=(hbm(), hbm(), hbm()),
        scratch_shapes=[
            pltpu.VMEM((col_devs, CAP, feature, cells), BF16),
            pltpu.VMEM((2, cols // 2, bins, rows), BF16),
            pltpu.SemaphoreType.DMA((peers,)), pltpu.SemaphoreType.DMA((peers,)),
            pltpu.SemaphoreType.DMA((peers,)), pltpu.SemaphoreType.DMA((peers,)),
            pltpu.SemaphoreType.DMA((2,)),
            pltpu.SemaphoreType.DMA((2,)), pltpu.SemaphoreType.DMA((2,)),
        ],
        compiler_params=pltpu.CompilerParams(
            collective_id=0, has_side_effects=True, vmem_limit_bytes=VMEM_LIMIT),
    )(idx, inv, ids, tiles_t, cot_t)


BAND = 8


def compute_kernel(cols, rows, ids_ref, pair_ref, recv_ref, cot_ref, mir_ref, wt_ref, gain_ref, bias_ref,
                   wg_ref, wu_ref, wo_ref, wd_ref,
                   gp_ref, g_ref, hs_ref, hl_ref, acc_ref,
                   s_ref, d_ref, z_ref, ag_ref, au_ref, ao_ref, ad_ref, at_ref, an_ref):
    step = pl.program_id(0)
    col_devs = recv_ref.shape[0]
    width = gain_ref.shape[1]
    hidden = wg_ref.shape[1]
    squares, feature, cells_sq = s_ref.shape
    sq_cols = cols // SQ
    cells = BAND * cols

    @pl.when(step == 0)
    def _():
        for ref in (s_ref, ag_ref, au_ref, ao_ref, ad_ref, at_ref, an_ref):
            ref[...] = jnp.zeros(ref.shape, F32)

        def land(n, carry):
            d, k = n // CAP, lax.rem(n, CAP)
            square = ids_ref[d, 0, k]

            @pl.when(square >= 0)
            def _():
                s_ref[square] += recv_ref[d, k].astype(F32)
            return carry

        lax.fori_loop(0, col_devs * CAP, land, 0)

        def own(j, carry):
            d_ref[pl.ds(j, rows, stride=cols), :] = cot_ref[j].astype(F32).T
            return carry

        lax.fori_loop(0, cols, own, 0)

        def mirrored(n, carry):
            at = pl.multiple_of(n * rows, rows)
            d_ref[pl.ds(at, rows), :] += mir_ref[n // (cols // 2), lax.rem(n, cols // 2)].astype(F32).T
            return carry

        lax.fori_loop(0, cols, mirrored, 0)

    row0 = step * BAND
    first = row0 // SQ * sq_cols
    at = pl.multiple_of(lax.rem(row0, SQ) * SQ, BAND * SQ)
    w_t = wt_ref[...]
    pieces = [s_ref[first + d, :, pl.ds(at, BAND * SQ)].astype(BF16) for d in range(sq_cols)]
    proj = jnp.concatenate(
        [tn(piece, w_t).reshape(BAND, SQ, width) for piece in pieces], axis=1).reshape(cells, width)
    z1 = pair_ref[...].reshape(cells, width) + proj
    gain, bias = gain_ref[...], bias_ref[...]
    mean = jnp.mean(z1, axis=1, keepdims=True)
    centered = z1 - mean
    rdev = lax.rsqrt(jnp.mean(centered * centered, axis=1, keepdims=True) + 1e-5)
    xhat = centered * rdev
    normed = (xhat * gain + bias).astype(BF16)
    base = pl.multiple_of(step * cells, cells)
    dheads = d_ref[pl.ds(base, cells), :].astype(BF16)
    wd = wd_ref[...]
    dz2 = nn(dheads, wd)
    dzl = dz2.astype(BF16)
    normed_t = normed.T
    dzl_t = dzl.T
    z2 = z1
    dnorm = jnp.zeros((cells, width), F32)
    part = 256
    for k in range(hidden // part):
        span = slice(k * part, (k + 1) * part)
        gate = nn(normed, wg_ref[:, span])
        up = nn(normed, wu_ref[:, span])
        dhid = nt(dzl, wo_ref[span, :])
        s = 0.5 * jnp.tanh(0.5 * gate) + 0.5
        swish = gate * s
        hid = (swish * up).astype(BF16)
        dup = (dhid * swish).astype(BF16)
        dgate = (dhid * up * (s + swish * (1.0 - s))).astype(BF16)
        z2 = z2 + nn(hid, wo_ref[span, :])
        dnorm = dnorm + nt(dgate, wg_ref[:, span]) + nt(dup, wu_ref[:, span])
        ao_ref[:, span] += nn(dzl_t, hid)
        ag_ref[:, span] += nn(normed_t, dgate)
        au_ref[:, span] += nn(normed_t, dup)
    z_ref[pl.ds(base, cells), :] = z2
    z2_low = z2.astype(BF16)
    heads_t = nt(wd, z2_low).astype(BF16)
    for k in range(cells // 128):
        hs_ref[k] = heads_t[:, k * 128:(k + 1) * 128]
    ad_ref[...] += tn(dheads, z2_low)
    an_ref[0] += jnp.sum((dnorm * xhat).reshape(cells // 8, 8, width), axis=0)
    an_ref[1] += jnp.sum(dnorm.reshape(cells // 8, 8, width), axis=0)
    dx = dnorm * gain
    grad = dz2 + (dx - jnp.mean(dx, axis=1, keepdims=True)
                  - xhat * jnp.mean(dx * xhat, axis=1, keepdims=True)) * rdev
    grad3 = grad.reshape(BAND, cols, width)
    gp_ref[...] = grad3
    total = jnp.zeros((feature, width), F32)
    for d in range(sq_cols):
        dproj = grad3[:, d * SQ:(d + 1) * SQ, :].reshape(BAND * SQ, width).astype(BF16)
        g_ref[first + d, :, pl.ds(at, BAND * SQ)] = nt(w_t, dproj).astype(BF16)
        total = total + nn(pieces[d], dproj)
    at_ref[...] += total

    @pl.when(step == pl.num_programs(0) - 1)
    def _():
        def local(j, carry):
            zj = z_ref[pl.ds(j, rows, stride=cols), :].astype(BF16)
            hl_ref[j] = nt(wd, zj).astype(BF16)
            return carry

        lax.fori_loop(0, cols, local, 0)
        for k in range(hidden // width):
            span = slice(k * width, (k + 1) * width)
            acc_ref[k * width:(k + 1) * width, :] = ag_ref[:, span]
            acc_ref[hidden + k * width:hidden + (k + 1) * width, :] = au_ref[:, span]
            acc_ref[2 * hidden + k * width:2 * hidden + (k + 1) * width, :] = ao_ref[:, span].T
        base3 = 3 * hidden
        bins = wd.shape[0]
        acc_ref[base3:base3 + bins, :] = ad_ref[...]
        acc_ref[base3 + bins:base3 + bins + feature, :] = at_ref[...]
        tail = base3 + bins + feature
        acc_ref[tail:tail + 8, :] = an_ref[0]
        acc_ref[tail + 8:tail + 16, :] = an_ref[1]
        acc_ref[tail + 16:, :] = jnp.zeros((ROWS_SUM - tail - 16, width), F32)


def compute(ids, pair, recv, cot_t, mir, w_t, gain, bias, w_gate, w_up, w_out, wd_t):
    rows, cols, width = pair.shape
    bins = wd_t.shape[0]
    feature, cells_sq = recv.shape[2:]
    hidden = w_gate.shape[1]
    squares = rows // SQ * (cols // SQ)
    whole = lambda x: pl.BlockSpec(x.shape, lambda i: (0,) * x.ndim, pipeline_mode=pl.Buffered(1))
    ops = (pair, recv, cot_t, mir, w_t, gain, bias, w_gate, w_up, w_out, wd_t)
    hs_step = BAND * cols // 128
    return pl.pallas_call(
        functools.partial(compute_kernel, cols, rows),
        name="pair_block",
        grid=(rows // BAND,),
        out_shape=(
            jax.ShapeDtypeStruct((rows, cols, width), F32),
            jax.ShapeDtypeStruct((squares, feature, cells_sq), BF16),
            jax.ShapeDtypeStruct((rows // 2, bins, 128), BF16),
            jax.ShapeDtypeStruct((cols, bins, rows), BF16),
            jax.ShapeDtypeStruct((ROWS_SUM, width), F32),
        ),
        in_specs=[smem(), pl.BlockSpec((BAND, cols, width), lambda i: (i, 0, 0))] + [whole(x) for x in ops[1:]],
        out_specs=(
            pl.BlockSpec((BAND, cols, width), lambda i: (i, 0, 0)),
            pl.BlockSpec((squares, feature, cells_sq), lambda i: (0, 0, 0)),
            pl.BlockSpec((hs_step, bins, 128), lambda i: (i, 0, 0)),
            pl.BlockSpec((cols, bins, rows), lambda i: (0, 0, 0)),
            pl.BlockSpec((ROWS_SUM, width), lambda i: (0, 0)),
        ),
        scratch_shapes=[
            pltpu.VMEM((squares, feature, cells_sq), F32),
            pltpu.VMEM((rows * cols, bins), F32),
            pltpu.VMEM((rows * cols, width), F32),
            pltpu.VMEM((width, hidden), F32),
            pltpu.VMEM((width, hidden), F32),
            pltpu.VMEM((width, hidden), F32),
            pltpu.VMEM((bins, width), F32),
            pltpu.VMEM((feature, width), F32),
            pltpu.VMEM((2, 8, width), F32),
        ],
        compiler_params=pltpu.CompilerParams(
            dimension_semantics=("arbitrary",), vmem_limit_bytes=VMEM_LIMIT),
    )(ids, *ops)


def return_kernel(row_devs, col_devs, scale, ids_ref, g_ref, hs_ref, acc_ref,
                  back_ref, mir_ref, sum_ref, sendbuf, low, rs_recv, cs_send, cs_recv, piece, chunk,
                  dma_send, dma_recv, own_sem, mir_send, mir_recv, a_send, a_recv, b_send, b_recv,
                  c_send, c_recv, d_send, d_recv):
    row, col = lax.axis_index("row"), lax.axis_index("col")
    shape, order = displacements(col_devs)
    barrier, count = greet(row, col, row_devs, col_devs, True)
    rows_chunk = ROWS_SUM // row_devs
    rows_piece = rows_chunk // col_devs
    low[...] = acc_ref[...].astype(BF16)

    def fill(d, carry):
        for k in range(CAP):
            sendbuf[d, k] = g_ref[jnp.maximum(ids_ref[d, 0, k], 0)]
        return carry

    lax.fori_loop(0, col_devs, fill, 0)
    greeted(row, col, barrier, count)

    def at_row(k):
        return lax.rem(row + k, row_devs)

    def part(r):
        return pl.ds(pl.multiple_of(r * rows_chunk, rows_chunk), rows_chunk)

    first = []
    for k in range(1, row_devs):
        to = at_row(k)
        first.append(pltpu.make_async_remote_copy(
            src_ref=low.at[part(to)], dst_ref=rs_recv.at[k - 1], send_sem=a_send.at[k - 1],
            recv_sem=a_recv.at[k - 1], device_id=(to, col), device_id_type=MESH))
    bulk = []
    for k, step in enumerate(order):
        to = moved(col, shape, step, 1)
        bulk.append(pltpu.make_async_remote_copy(
            src_ref=sendbuf.at[to], dst_ref=back_ref.at[col], send_sem=dma_send.at[k],
            recv_sem=dma_recv.at[k], device_id=(row, to), device_id_type=MESH))
    half = hs_ref.shape[0] // 2
    sources = (hs_ref.at[pl.ds(0, half)], hs_ref.at[pl.ds(half, half)])
    mirror = mirror_copies(row, col, sources, mir_ref, mir_send, mir_recv)
    own = pltpu.make_async_copy(sendbuf.at[col], back_ref.at[col], own_sem.at[0])

    for copy in first:
        copy.start()
    start_mirror(mirror)
    own.start()
    third = (len(bulk) + 2) // 3
    for copy in bulk[:third]:
        copy.start()

    for copy in first:
        copy.wait()
    total = acc_ref[part(row), :]
    for k in range(row_devs - 1):
        total = total + rs_recv[k].astype(F32)
    cs_send[...] = total.astype(BF16).reshape(cs_send.shape)
    second = []
    for k, step in enumerate(order):
        to = moved(col, shape, step, 1)
        second.append(pltpu.make_async_remote_copy(
            src_ref=cs_send.at[to], dst_ref=cs_recv.at[k], send_sem=b_send.at[k],
            recv_sem=b_recv.at[k], device_id=(row, to), device_id_type=MESH))
    for copy in second:
        copy.start()
    for copy in bulk[third:2 * third]:
        copy.start()
    for copy in second:
        copy.wait()
    mine = cs_send[col].astype(F32)
    for k in range(col_devs - 1):
        mine = mine + cs_recv[k].astype(F32)
    piece[...] = (mine * scale).astype(BF16)
    chunk[col] = piece[...]
    third_leg = []
    for k, step in enumerate(order):
        third_leg.append(pltpu.make_async_remote_copy(
            src_ref=piece, dst_ref=chunk.at[col], send_sem=c_send.at[k],
            recv_sem=c_recv.at[k], device_id=(row, moved(col, shape, step, 1)), device_id_type=MESH))
    for copy in third_leg:
        copy.start()
    for copy in bulk[2 * third:]:
        copy.start()
    for copy in third_leg:
        copy.wait()
    last = []
    for k in range(1, row_devs):
        last.append(pltpu.make_async_remote_copy(
            src_ref=chunk, dst_ref=sum_ref.at[row], send_sem=d_send.at[k - 1],
            recv_sem=d_recv.at[k - 1], device_id=(at_row(k), col), device_id_type=MESH))
    for copy in last:
        copy.start()
    own_sum = pltpu.make_async_copy(chunk, sum_ref.at[row], own_sem.at[1])
    own_sum.start()
    own_sum.wait()
    for copy in last:
        copy.wait()
    own.wait()
    wait_mirror(mirror, sources, mir_ref, mir_recv)
    for copy in bulk:
        copy.wait()


def give_back(row_devs, col_devs, scale, ids, g, hs, acc):
    squares, feature, cells = g.shape
    bins = hs.shape[1]
    peers = col_devs - 1
    rows_chunk = ROWS_SUM // row_devs
    rows_piece = rows_chunk // col_devs
    dma = lambda n: pltpu.SemaphoreType.DMA((n,))
    return pl.pallas_call(
        functools.partial(return_kernel, row_devs, col_devs, scale),
        name="give_back",
        out_shape=(
            jax.ShapeDtypeStruct((col_devs, CAP, feature, cells), BF16),
            jax.ShapeDtypeStruct((2, hs.shape[0] // 2, bins, 128), BF16),
            jax.ShapeDtypeStruct((row_devs, col_devs, rows_piece, 128), BF16),
        ),
        in_specs=[smem(), vmem(), vmem(), vmem()],
        out_specs=(hbm(), hbm(), hbm()),
        scratch_shapes=[
            pltpu.VMEM((col_devs, CAP, feature, cells), BF16),
            pltpu.VMEM((ROWS_SUM, 128), BF16),
            pltpu.VMEM((row_devs - 1, rows_chunk, 128), BF16),
            pltpu.VMEM((col_devs, rows_piece, 128), BF16),
            pltpu.VMEM((col_devs - 1, rows_piece, 128), BF16),
            pltpu.VMEM((rows_piece, 128), BF16),
            pltpu.VMEM((col_devs, rows_piece, 128), BF16),
            dma(peers), dma(peers), dma(2), dma(2), dma(2),
            dma(row_devs - 1), dma(row_devs - 1), dma(peers), dma(peers),
            dma(peers), dma(peers), dma(row_devs - 1), dma(row_devs - 1),
        ],
        compiler_params=pltpu.CompilerParams(
            collective_id=1, has_side_effects=True, vmem_limit_bytes=VMEM_LIMIT),
    )(ids, g, hs, acc)


def finish_kernel(hidden, slot_ref, back_ref, inv_ref, mir_ref, hl_ref, sum_ref,
                  tile_ref, log_ref, gt_ref, gg_ref, gu_ref, go_ref, gd_ref, gn_ref):
    step = pl.program_id(0)
    tile_ref[0] = (back_ref[0].astype(F32) * inv_ref[step]).astype(BF16)
    bins, lanes = hl_ref.shape[1:]
    low = lax.broadcasted_iota(jnp.int32, (bins, lanes), 1) < lanes // 2
    for k in range(mir_ref.shape[1]):
        a, b = mir_ref[0, k].astype(F32), mir_ref[1, k].astype(F32)
        even = jnp.where(low, a, pltpu.roll(b, lanes // 2, 1))
        odd = jnp.where(low, pltpu.roll(a, lanes // 2, 1), b)
        log_ref[2 * k] = (hl_ref[2 * k].astype(F32) + even).astype(BF16)
        log_ref[2 * k + 1] = (hl_ref[2 * k + 1].astype(F32) + odd).astype(BF16)

    @pl.when(step == 0)
    def _():
        width = sum_ref.shape[1]
        for k in range(hidden // width):
            span = slice(k * width, (k + 1) * width)
            gg_ref[:, span] = sum_ref[k * width:(k + 1) * width, :].astype(F32)
            gu_ref[:, span] = sum_ref[hidden + k * width:hidden + (k + 1) * width, :].astype(F32)
        go_ref[...] = sum_ref[2 * hidden:3 * hidden, :].astype(F32)
        at = 3 * hidden
        gd_ref[...] = sum_ref[at:at + gd_ref.shape[0], :].astype(F32)
        at += gd_ref.shape[0]
        gt_ref[...] = sum_ref[at:at + gt_ref.shape[0], :].astype(F32)
        at += gt_ref.shape[0]
        norm = sum_ref[at:at + 16, :].astype(F32)
        gn_ref[0:1, :] = jnp.sum(norm[0:8], axis=0, keepdims=True)
        gn_ref[1:2, :] = jnp.sum(norm[8:16], axis=0, keepdims=True)


def finish(hidden, slot_of, inv, back, mir, hl, sums):
    slots = slot_of.shape[0]
    feature, cells = back.shape[1:]
    cols, bins, rows = hl.shape
    width = sums.shape[1]
    per = cols // slots
    const = lambda shape: pl.BlockSpec(shape, lambda i, s: (0,) * len(shape))
    outs = [((slots, feature, cells), BF16), ((cols, bins, rows), BF16), ((feature, width), F32),
            ((width, hidden), F32), ((width, hidden), F32), ((hidden, width), F32), ((bins, width), F32),
            ((2, width), F32)]
    return pl.pallas_call(
        functools.partial(finish_kernel, hidden),
        name="finish",
        grid_spec=pltpu.PrefetchScalarGridSpec(
            num_scalar_prefetch=1,
            grid=(slots,),
            in_specs=[
                pl.BlockSpec((1, feature, cells), lambda i, s: (s[i], 0, 0)),
                pl.BlockSpec(memory_space=pltpu.SMEM),
                pl.BlockSpec((2, per // 2, bins, rows), lambda i, s: (0, i, 0, 0)),
                pl.BlockSpec((per, bins, rows), lambda i, s: (i, 0, 0)),
                const(sums.shape),
            ],
            out_specs=[
                pl.BlockSpec((1, feature, cells), lambda i, s: (i, 0, 0)),
                pl.BlockSpec((per, bins, rows), lambda i, s: (i, 0, 0)),
            ] + [const(shape) for shape, _ in outs[2:]],
        ),
        out_shape=[jax.ShapeDtypeStruct(shape, kind) for shape, kind in outs],
        compiler_params=pltpu.CompilerParams(
            dimension_semantics=("arbitrary",), vmem_limit_bytes=VMEM_LIMIT),
    )(slot_of, back, inv, mir, hl, sums)


def per_device(pair, logit_cotangent, tiles, tile_target, tile_square, tile_count, w_template,
               transition_norm_gain, transition_norm_bias, w_gate, w_up, w_out, w_dist):
    row_devs = lax.axis_size("row")
    col_devs = lax.axis_size("col")
    rows, cols, width = pair.shape
    length = rows * row_devs
    slots, cells_sq, feature = tiles.shape
    hidden = w_gate.shape[1]
    tiles_t = jnp.transpose(tiles, (0, 2, 1))
    cot_t = jnp.transpose(logit_cotangent, (1, 2, 0))
    target = tile_target[:, 0]
    places = jnp.arange(slots, dtype=jnp.int32)
    rank = jnp.sum((target[:, None] == target[None, :]) & (places[None, :] < places[:, None]),
                   axis=1, dtype=jnp.int32)
    slot_of = target * CAP + rank
    inv_count = 1.0 / tile_count.astype(F32)
    chosen = slot_of[None, :] == jnp.arange(col_devs * CAP, dtype=jnp.int32)[:, None]
    picked = chosen.astype(jnp.int32)
    idx = jnp.sum(picked * places[None, :], axis=1).reshape(col_devs, CAP)
    send_inv = jnp.sum(jnp.where(chosen, inv_count[None, :], 0.0), axis=1).reshape(col_devs, CAP)
    send_ids = (jnp.sum(picked * (tile_square + 1)[None, :], axis=1) - 1).reshape(col_devs, CAP)
    ids = jnp.broadcast_to(jnp.pad(send_ids, ((0, 0), (0, 128 - CAP)))[:, None, :], (col_devs, 8, 128))

    recv, got, mir = exchange(row_devs, col_devs, idx, send_inv, ids, tiles_t, cot_t)
    grad_pair, g, hs, hl, acc = compute(
        got, pair, recv, cot_t, mir, w_template, transition_norm_gain[None, :],
        transition_norm_bias[None, :], w_gate, w_up, w_out, w_dist.T)
    back, mir_heads, sums = give_back(row_devs, col_devs, 1.0 / length, got, g, hs, acc)
    grad_tiles_t, logits_t, g_template, g_gate, g_up, g_out, g_dist_t, g_norm = finish(
        hidden, slot_of, inv_count, back.reshape(col_devs * CAP, feature, cells_sq), mir_heads, hl,
        sums.reshape(ROWS_SUM, width))
    return (
        jnp.transpose(logits_t, (2, 0, 1)),
        grad_pair,
        jnp.transpose(grad_tiles_t, (0, 2, 1)),
        g_template,
        g_norm[0],
        g_norm[1],
        g_gate,
        g_up,
        g_out,
        g_dist_t.T,
    )


def solution(mesh):
    return jax.shard_map(
        per_device,
        mesh=mesh,
        in_specs=(
            P("row", "col", None),
            P("row", "col", None),
            P(("row", "col"), None, None),
            P(("row", "col"), None),
            P(("row", "col")),
            P(("row", "col")),
            P(), P(), P(), P(), P(), P(), P(),
        ),
        out_specs=(
            P("row", "col", None),
            P("row", "col", None),
            P(("row", "col"), None, None),
            P(), P(), P(), P(), P(), P(), P(),
        ),
        check_vma=False,
    )
```

time: 961 us -> 307 us (0.32)
  the two profiles are of different devices: /device:TPU:1 before, /device:TPU:15 now
where the time goes in v1:
time: 307 us; the launch traced here: 304 us
  Pallas kernels  297 us (97%)
  local copies, waits for them, and re-layouts  3.37 us (1%)
    pallas_call x1, Pallas kernels, give_back(): pl.pallas_call(functools.partial(return_kernel, row_devs, col_devs, scale...  112 us
    pallas_call x1, Pallas kernels, exchange(): pl.pallas_call(functools.partial(exchange_kernel, row_devs, col_devs), na...  106 us
    pallas_call x1, Pallas kernels, compute(): pl.pallas_call(functools.partial(compute_kernel, cols, rows), name='pair_...  67 us
    pallas_call x1, Pallas kernels, finish(): pl.pallas_call(functools.partial(finish_kernel, hidden), name='finish', g...  11.7 us

profile of v1, /device:TPU:15, one launch (start us, length us, event | category | flops | bytes accessed | tf_op | source)
XLA Modules:
  0.0 303.8 jit_solution(15887284933689665533)
XLA Ops:
  0.6 0.7 convert_divide_fusion.inv_ref
  1.3 0.0 copy-start.1
  1.3 0.9 convert_reduce_fusion
  2.2 0.7 multiply_add_fusion
  2.9 0.0 copy-start
  2.9 0.1 select_reduce_fusion.1
  3.0 0.1 select_reduce_fusion
  3.1 0.1 sub.7
  3.2 0.7 reshape.49.inv_ref
  3.9 0.7 reshape.48.idx_ref
  4.6 0.6 broadcast_in_dim.20.ids_ref
  5.2 106.1 %exchange.1 = (bf16[16,2,64,1024]{3,2,1,0:T(8,128)(2,1)}, s32[16,8,128]{2,1,0:T(8,128)}, bf16[2,32,64,128]{3,2,1,0:T(8,128)(2,1)}) custom-call(s32[16,2]{1,0:T(8,128)} %reshape.48.idx_ref, f32[16,2]{1,0:T(8,128)} %reshape.49.inv_ref, s32[16,8,128]{2,1,0:T(8,128)} %broadcast_in_dim.20.ids_ref, bf16[16,64,1024]{2,1,0:T(8,128)(2,1)} %bitcast.19, ...), custom_call_target="tpu_custom_call" | custom-call | tf_op jit(solution)/shard_map/exchange/pallas_call | solution.py:171
  111.3 67.0 %pair_block.1 = (f32[128,64,128]{2,1,0:T(8,128)}, bf16[8,64,1024]{2,1,0:T(8,128)(2,1)}, bf16[64,64,128]{2,1,0:T(8,128)(2,1)}, bf16[64,64,128]{2,1,0:T(8,128)(2,1)}, f32[2048,128]{1,0:T(8,128)}) custom-call(s32[16,8,128]{2,1,0:T(8,128)} %get-tuple-element.29.ids_ref, f32[128,64,128]{2,1,0:T(8,128)} %pair_ref.1, ...), custom_call_target="tpu_custom_call" | custom-call | tf_op jit(solution)/shard_map/pair_block/pallas_call | solution.py:329
  178.3 0.0 copy-done.1
  178.3 0.0 copy-done
  178.3 112.5 %give_back.1 = (bf16[16,2,64,1024]{3,2,1,0:T(8,128)(2,1)}, bf16[2,32,64,128]{3,2,1,0:T(8,128)(2,1)}, bf16[8,16,16,128]{3,2,1,0:T(8,128)(2,1)}) custom-call(s32[16,8,128]{2,1,0:T(8,128)} %get-tuple-element.29.ids_ref, bf16[8,64,1024]{2,1,0:T(8,128)(2,1)} %get-tuple-element.32.g_ref, bf16[64,64,128]{2,1,0:T(8,128)(2,1)} %get-tuple-element.33.hs_ref, ...), custom_call_target="tpu_custom_call" | custom-call | tf_op jit(solution)/shard_map/give_back/pallas_call | solution.py:473
  290.8 11.7 %finish.1 = (bf16[16,64,1024]{2,1,0:T(8,128)(2,1)}, bf16[64,64,128]{2,1,0:T(8,128)(2,1)}, f32[64,128]{1,0:T(8,128)}, f32[128,512]{1,0:T(8,128)}, f32[128,512]{1,...) custom-call(s32[16]{0:T(128)} %copy-done, bf16[32,64,1024]{2,1,0:T(8,128)(2,1)} %bitcast.16, ...), custom_call_target="tpu_custom_call" | custom-call | tf_op jit(solution)/shard_map/finish/pallas_call | solution.py:541
  302.5 1.3 slice_bitcast_fusion
  (2 shorter events, 0.0 us)
Async XLA Ops:
  1.3 177.0 %copy-start.1 = (f32[16]{0:T(128)}, f32[16]{0:T(128)S(1)}, u32[]{:S(2)}) copy-start(f32[16]{0:T(128)S(1)} %convert_divide_fusion.inv_ref) | copy-start | bytes 196
  2.9 175.4 %copy-start = (s32[16]{0:T(128)}, s32[16]{0:T(128)S(1)}, u32[]{:S(2)}) copy-start(s32[16]{0:T(128)S(1)} %get-tuple-element.52.slot_ref) | copy-start | bytes 196

commit v2 on v1

--- a/solution.py
+++ b/solution.py
@@ -55,79 +55,135 @@
     return y * zs + z
 
 
-def mirror_copies(row, col, src, dst, send_sem, recv_sem):
-    out = []
-    for h in (0, 1):
-        to_row, to_col = col // 2, 2 * row + h
-        here = jnp.logical_and(to_row == row, to_col == col)
-        slot = lax.rem(col, 2)
-        remote = pltpu.make_async_remote_copy(
-            src_ref=src[h], dst_ref=dst.at[slot], send_sem=send_sem.at[h],
-            recv_sem=recv_sem.at[slot], device_id=(to_row, to_col), device_id_type=MESH)
-        local = pltpu.make_async_copy(src[h], dst.at[slot], recv_sem.at[slot])
-        out.append((here, remote, local))
-    return out
-
-
-def start_mirror(copies):
-    for here, remote, local in copies:
-        @pl.when(jnp.logical_not(here))
-        def _():
-            remote.start()
-
-        @pl.when(here)
-        def _():
-            local.start()
-
-
-def wait_mirror(copies, src, dst, recv_sem):
-    for h, (here, remote, local) in enumerate(copies):
-        @pl.when(jnp.logical_not(here))
-        def _():
-            remote.wait_send()
-
-        pltpu.make_async_copy(src[h], dst.at[h], recv_sem.at[h]).wait()
-
-
-def greet(row, col, row_devs, col_devs, rows_too):
+class Place:
+    def __init__(self, row_devs, col_devs):
+        self.row, self.col = lax.axis_index("row"), lax.axis_index("col")
+        self.xs, self.zs = row_devs // 2, col_devs // (row_devs // 2)
+        self.x, self.k = self.row // 2, lax.rem(self.row, 2)
+        self.y, self.z = self.col // self.zs, lax.rem(self.col, self.zs)
+
+    def turn(self, value, by):
+        return lax.rem(value + by, self.xs) if self.xs > 1 else value
+
+
+class Mirror:
+    def __init__(self, place, src, first, second, dst, sems):
+        self.p, self.src, self.first, self.second, self.dst = place, src, first, second, dst
+        self.s1, self.r1, self.s2, self.r2, self.s3, self.r3, self.own = sems
+
+    def along_x(self, source, target, send, recv):
+        p = self.p
+        copies = []
+        for n in range(1, p.xs):
+            to = p.turn(p.x, n)
+            copies.append(pltpu.make_async_remote_copy(
+                src_ref=source(to), dst_ref=target.at[p.x], send_sem=send.at[n - 1], recv_sem=recv.at[n - 1],
+                device_id=(2 * to + p.k, p.col), device_id_type=MESH))
+        return copies
+
+    def start_1(self):
+        p = self.p
+        self.copies = self.along_x(lambda to: self.src.at[:, to], self.first, self.s1, self.r1)
+        for copy in self.copies:
+            copy.start()
+        self.local = pltpu.make_async_copy(self.src.at[:, p.x], self.first.at[p.x], self.own.at[0])
+        self.local.start()
+
+    def finish(self):
+        self.local.wait()
+        for copy in self.copies:
+            copy.wait()
+
+    def start_2(self):
+        p = self.p
+        self.plan = []
+        for n in range(p.xs):
+            to_y = p.turn(p.y, n)
+            for h in (0, 1):
+                to_z, to_k = 2 * p.k + h, p.z // 2
+                source, target = self.first.at[to_y, h], self.second.at[p.y, lax.rem(p.z, 2)]
+                slot = 2 * n + lax.rem(p.z, 2)
+                remote = pltpu.make_async_remote_copy(
+                    src_ref=source, dst_ref=target, send_sem=self.s2.at[2 * n + h], recv_sem=self.r2.at[slot],
+                    device_id=(2 * p.x + to_k, to_y * p.zs + to_z), device_id_type=MESH)
+                if n == 0:
+                    here = jnp.logical_and(to_k == p.k, to_z == p.z)
+                    local = pltpu.make_async_copy(source, target, self.r2.at[slot])
+                    start_one(here, remote, local)
+                    self.plan.append((here, remote))
+                else:
+                    remote.start()
+                    self.plan.append((None, remote))
+
+    def finish_2(self):
+        for i, (here, remote) in enumerate(self.plan):
+            if here is None:
+                remote.wait_send()
+            else:
+                @pl.when(jnp.logical_not(here))
+                def _():
+                    remote.wait_send()
+            ref = self.second.at[0, 0]
+            pltpu.make_async_copy(ref, ref, self.r2.at[i]).wait()
+
+    def start_3(self):
+        p = self.p
+        self.copies = self.along_x(lambda to: self.second.at[to], self.dst, self.s3, self.r3)
+        for copy in self.copies:
+            copy.start()
+        self.local = pltpu.make_async_copy(self.second.at[p.x], self.dst.at[p.x], self.own.at[1])
+        self.local.start()
+
+
+def start_one(here, remote, local):
+    @pl.when(jnp.logical_not(here))
+    def _():
+        remote.start()
+
+    @pl.when(here)
+    def _():
+        local.start()
+
+
+def mirror_sems(row_devs):
+    xs = row_devs // 2
+    dma = lambda n: pltpu.SemaphoreType.DMA((n,))
+    return [dma(max(xs - 1, 1)), dma(max(xs - 1, 1)), dma(2 * xs), dma(2 * xs),
+            dma(max(xs - 1, 1)), dma(max(xs - 1, 1)), dma(2)]
+
+
+def greet(p, row_devs, col_devs):
     barrier = pltpu.get_barrier_semaphore()
+    peers = 0
+    for n in range(1, col_devs):
+        pl.semaphore_signal(barrier, inc=1, device_id=(p.row, lax.rem(p.col + n, col_devs)), device_id_type=MESH)
+        peers += 1
+    for n in range(1, row_devs):
+        pl.semaphore_signal(barrier, inc=1, device_id=(lax.rem(p.row + n, row_devs), p.col), device_id_type=MESH)
+        peers += 1
+    for n in range(1, col_devs):
+        pl.semaphore_signal(
+            barrier, inc=1, device_id=(2 * p.x + 1 - p.k, lax.rem(p.col + n, col_devs)), device_id_type=MESH)
+        peers += 1
+    return lambda: pl.semaphore_wait(barrier, peers)
+
+
+def exchange_kernel(row_devs, col_devs, idx_ref, inv_ref, ids_ref, tiles_ref, cot_ref,
+                    recv_ref, got_ref, mir_ref, sendbuf, pack, first, second, dma_send, dma_recv,
+                    id_send, id_recv, own_sem, *mirror_sem):
+    p = Place(row_devs, col_devs)
+    row, col = p.row, p.col
     shape, order = displacements(col_devs)
-    for step in order:
-        pl.semaphore_signal(barrier, inc=1, device_id=(row, moved(col, shape, step, 1)), device_id_type=MESH)
-    count = len(order)
-    if rows_too:
-        for k in range(1, row_devs):
-            pl.semaphore_signal(
-                barrier, inc=1, device_id=(lax.rem(row + k, row_devs), col), device_id_type=MESH)
-        count += row_devs - 1
-    for h in (0, 1):
-        to_row, to_col = col // 2, 2 * row + h
-
-        @pl.when(jnp.logical_not(jnp.logical_and(to_row == row, to_col == col)))
-        def _():
-            pl.semaphore_signal(barrier, inc=1, device_id=(to_row, to_col), device_id_type=MESH)
-    return barrier, count
-
-
-def greeted(row, col, barrier, count):
-    here = (col // 2 == row).astype(jnp.int32)
-    pl.semaphore_wait(barrier, count + 2 - here)
-
-
-def exchange_kernel(row_devs, col_devs, idx_ref, inv_ref, ids_ref, tiles_ref, cot_ref,
-                    recv_ref, got_ref, mir_ref, sendbuf, pack, dma_send, dma_recv, id_send, id_recv,
-                    own_sem, mir_send, mir_recv):
-    row, col = lax.axis_index("row"), lax.axis_index("col")
-    shape, order = displacements(col_devs)
-    barrier, count = greet(row, col, row_devs, col_devs, False)
+    greeted = greet(p, row_devs, col_devs)
 
     bins, lanes = cot_ref.shape[1:]
     low = lax.broadcasted_iota(jnp.int32, (bins, lanes), 1) < lanes // 2
 
     def pack_pair(k, carry):
         a, b = cot_ref[2 * k].astype(F32), cot_ref[2 * k + 1].astype(F32)
-        pack[0, k] = jnp.where(low, a, pltpu.roll(b, lanes // 2, 1)).astype(BF16)
-        pack[1, k] = jnp.where(low, pltpu.roll(a, lanes // 2, 1), b).astype(BF16)
+        m, t = k // pack.shape[2], lax.rem(k, pack.shape[2])
+        pack[0, m, t] = jnp.where(low, a, pltpu.roll(b, lanes // 2, 1)).astype(BF16)
+        pack[1, m, t] = jnp.where(low, pltpu.roll(a, lanes // 2, 1), b).astype(BF16)
         return carry
 
     lax.fori_loop(0, cot_ref.shape[0] // 2, pack_pair, 0)
@@ -138,54 +194,64 @@
         return carry
 
     lax.fori_loop(0, col_devs, fill, 0)
-    greeted(row, col, barrier, count)
-
-    mirror = mirror_copies(row, col, (pack.at[0], pack.at[1]), mir_ref, mir_send, mir_recv)
-    start_mirror(mirror)
-    copies = []
+    greeted()
+
+    mirror = Mirror(p, pack, first, second, mir_ref, mirror_sem)
+    mirror.start_1()
+    names, bulk = [], []
     for k, step in enumerate(order):
         to = moved(col, shape, step, 1)
-        copies.append(pltpu.make_async_remote_copy(
+        names.append(pltpu.make_async_remote_copy(
+            src_ref=ids_ref.at[to], dst_ref=got_ref.at[col], send_sem=id_send.at[k],
+            recv_sem=id_recv.at[k], device_id=(row, to), device_id_type=MESH))
+        bulk.append(pltpu.make_async_remote_copy(
             src_ref=sendbuf.at[to], dst_ref=recv_ref.at[col], send_sem=dma_send.at[k],
             recv_sem=dma_recv.at[k], device_id=(row, to), device_id_type=MESH))
-        copies.append(pltpu.make_async_remote_copy(
-            src_ref=ids_ref.at[to], dst_ref=got_ref.at[col], send_sem=id_send.at[k],
-            recv_sem=id_recv.at[k], device_id=(row, to), device_id_type=MESH))
-    for copy in copies:
-        copy.start()
     own = pltpu.make_async_copy(sendbuf.at[col], recv_ref.at[col], own_sem.at[0])
     own_id = pltpu.make_async_copy(ids_ref.at[col], got_ref.at[col], own_sem.at[1])
     own.start()
     own_id.start()
+    ahead = len(bulk) * 2 // 5
+    for copy in names + bulk[:ahead]:
+        copy.start()
+    mirror.finish()
+    mirror.start_2()
+    for copy in bulk[ahead:]:
+        copy.start()
+    mirror.finish_2()
+    mirror.start_3()
     own.wait()
     own_id.wait()
-    for copy in copies:
+    for copy in names:
         copy.wait()
-    wait_mirror(mirror, (pack.at[0], pack.at[1]), mir_ref, mir_recv)
+    mirror.finish()
+    for copy in bulk:
+        copy.wait()
 
 
 def exchange(row_devs, col_devs, idx, inv, ids, tiles_t, cot_t):
     slots, feature, cells = tiles_t.shape
     cols, bins, rows = cot_t.shape
-    peers = col_devs - 1
+    peers, xs = col_devs - 1, row_devs // 2
     return pl.pallas_call(
         functools.partial(exchange_kernel, row_devs, col_devs),
         name="exchange",
         out_shape=(
             jax.ShapeDtypeStruct((col_devs, CAP, feature, cells), BF16),
             jax.ShapeDtypeStruct((col_devs, 8, 128), jnp.int32),
-            jax.ShapeDtypeStruct((2, cols // 2, bins, rows), BF16),
+            jax.ShapeDtypeStruct((xs, 2, cols // 2 // xs, bins, rows), BF16),
         ),
         in_specs=[smem(), smem(), vmem(), vmem(), vmem()],
         out_specs=(hbm(), hbm(), hbm()),
         scratch_shapes=[
             pltpu.VMEM((col_devs, CAP, feature, cells), BF16),
-            pltpu.VMEM((2, cols // 2, bins, rows), BF16),
+            pltpu.VMEM((2, xs, cols // 2 // xs, bins, rows), BF16),
+            pltpu.VMEM((xs, 2, cols // 2 // xs, bins, rows), BF16),
+            pltpu.VMEM((xs, 2, cols // 2 // xs, bins, rows), BF16),
             pltpu.SemaphoreType.DMA((peers,)), pltpu.SemaphoreType.DMA((peers,)),
             pltpu.SemaphoreType.DMA((peers,)), pltpu.SemaphoreType.DMA((peers,)),
             pltpu.SemaphoreType.DMA((2,)),
-            pltpu.SemaphoreType.DMA((2,)), pltpu.SemaphoreType.DMA((2,)),
-        ],
+        ] + mirror_sems(row_devs),
         compiler_params=pltpu.CompilerParams(
             collective_id=0, has_side_effects=True, vmem_limit_bytes=VMEM_LIMIT),
     )(idx, inv, ids, tiles_t, cot_t)
@@ -230,7 +296,8 @@
 
         def mirrored(n, carry):
             at = pl.multiple_of(n * rows, rows)
-            d_ref[pl.ds(at, rows), :] += mir_ref[n // (cols // 2), lax.rem(n, cols // 2)].astype(F32).T
+            d_ref[pl.ds(at, rows), :] += mir_ref[
+                lax.rem(n, cols // 2) // mir_ref.shape[2], n // (cols // 2), lax.rem(n, mir_ref.shape[2])].astype(F32).T
             return carry
 
         lax.fori_loop(0, cols, mirrored, 0)
@@ -363,11 +430,12 @@
 
 def return_kernel(row_devs, col_devs, scale, ids_ref, g_ref, hs_ref, acc_ref,
                   back_ref, mir_ref, sum_ref, sendbuf, low, rs_recv, cs_send, cs_recv, piece, chunk,
-                  dma_send, dma_recv, own_sem, mir_send, mir_recv, a_send, a_recv, b_send, b_recv,
-                  c_send, c_recv, d_send, d_recv):
-    row, col = lax.axis_index("row"), lax.axis_index("col")
+                  m_first, m_second, dma_send, dma_recv, own_sem, a_send, a_recv, b_send, b_recv,
+                  c_send, c_recv, d_send, d_recv, *mirror_sem):
+    p = Place(row_devs, col_devs)
+    row, col = p.row, p.col
     shape, order = displacements(col_devs)
-    barrier, count = greet(row, col, row_devs, col_devs, True)
+    greeted = greet(p, row_devs, col_devs)
     rows_chunk = ROWS_SUM // row_devs
     rows_piece = rows_chunk // col_devs
     low[...] = acc_ref[...].astype(BF16)
@@ -378,7 +446,7 @@
         return carry
 
     lax.fori_loop(0, col_devs, fill, 0)
-    greeted(row, col, barrier, count)
+    greeted()
 
     def at_row(k):
         return lax.rem(row + k, row_devs)
@@ -398,19 +466,19 @@
         bulk.append(pltpu.make_async_remote_copy(
             src_ref=sendbuf.at[to], dst_ref=back_ref.at[col], send_sem=dma_send.at[k],
             recv_sem=dma_recv.at[k], device_id=(row, to), device_id_type=MESH))
-    half = hs_ref.shape[0] // 2
-    sources = (hs_ref.at[pl.ds(0, half)], hs_ref.at[pl.ds(half, half)])
-    mirror = mirror_copies(row, col, sources, mir_ref, mir_send, mir_recv)
+    mirror = Mirror(p, hs_ref, m_first, m_second, mir_ref, mirror_sem)
     own = pltpu.make_async_copy(sendbuf.at[col], back_ref.at[col], own_sem.at[0])
 
+    mirror.start_1()
     for copy in first:
         copy.start()
-    start_mirror(mirror)
     own.start()
     third = (len(bulk) + 2) // 3
     for copy in bulk[:third]:
         copy.start()
 
+    mirror.finish()
+    mirror.start_2()
     for copy in first:
         copy.wait()
     total = acc_ref[part(row), :]
@@ -427,6 +495,8 @@
         copy.start()
     for copy in bulk[third:2 * third]:
         copy.start()
+    mirror.finish_2()
+    mirror.start_3()
     for copy in second:
         copy.wait()
     mine = cs_send[col].astype(F32)
@@ -458,7 +528,7 @@
     for copy in last:
         copy.wait()
     own.wait()
-    wait_mirror(mirror, sources, mir_ref, mir_recv)
+    mirror.finish()
     for copy in bulk:
         copy.wait()
 
@@ -466,7 +536,9 @@
 def give_back(row_devs, col_devs, scale, ids, g, hs, acc):
     squares, feature, cells = g.shape
     bins = hs.shape[1]
-    peers = col_devs - 1
+    peers, xs = col_devs - 1, row_devs // 2
+    slices = (xs, 2, hs.shape[0] // 2 // xs, bins, 128)
+    hs = hs.reshape(2, xs, slices[2], bins, 128)
     rows_chunk = ROWS_SUM // row_devs
     rows_piece = rows_chunk // col_devs
     dma = lambda n: pltpu.SemaphoreType.DMA((n,))
@@ -475,7 +547,7 @@
         name="give_back",
         out_shape=(
             jax.ShapeDtypeStruct((col_devs, CAP, feature, cells), BF16),
-            jax.ShapeDtypeStruct((2, hs.shape[0] // 2, bins, 128), BF16),
+            jax.ShapeDtypeStruct(slices, BF16),
             jax.ShapeDtypeStruct((row_devs, col_devs, rows_piece, 128), BF16),
         ),
         in_specs=[smem(), vmem(), vmem(), vmem()],
@@ -488,10 +560,12 @@
             pltpu.VMEM((col_devs - 1, rows_piece, 128), BF16),
             pltpu.VMEM((rows_piece, 128), BF16),
             pltpu.VMEM((col_devs, rows_piece, 128), BF16),
-            dma(peers), dma(peers), dma(2), dma(2), dma(2),
+            pltpu.VMEM(slices, BF16),
+            pltpu.VMEM(slices, BF16),
+            dma(peers), dma(peers), dma(2),
             dma(row_devs - 1), dma(row_devs - 1), dma(peers), dma(peers),
             dma(peers), dma(peers), dma(row_devs - 1), dma(row_devs - 1),
-        ],
+        ] + mirror_sems(row_devs),
         compiler_params=pltpu.CompilerParams(
             collective_id=1, has_side_effects=True, vmem_limit_bytes=VMEM_LIMIT),
     )(ids, g, hs, acc)
@@ -503,8 +577,8 @@
     tile_ref[0] = (back_ref[0].astype(F32) * inv_ref[step]).astype(BF16)
     bins, lanes = hl_ref.shape[1:]
     low = lax.broadcasted_iota(jnp.int32, (bins, lanes), 1) < lanes // 2
-    for k in range(mir_ref.shape[1]):
-        a, b = mir_ref[0, k].astype(F32), mir_ref[1, k].astype(F32)
+    for k in range(mir_ref.shape[2]):
+        a, b = mir_ref[0, 0, k].astype(F32), mir_ref[0, 1, k].astype(F32)
         even = jnp.where(low, a, pltpu.roll(b, lanes // 2, 1))
         odd = jnp.where(low, pltpu.roll(a, lanes // 2, 1), b)
         log_ref[2 * k] = (hl_ref[2 * k].astype(F32) + even).astype(BF16)
@@ -534,6 +608,7 @@
     cols, bins, rows = hl.shape
     width = sums.shape[1]
     per = cols // slots
+    deep = mir.shape[2] // (per // 2)
     const = lambda shape: pl.BlockSpec(shape, lambda i, s: (0,) * len(shape))
     outs = [((slots, feature, cells), BF16), ((cols, bins, rows), BF16), ((feature, width), F32),
             ((width, hidden), F32), ((width, hidden), F32), ((hidden, width), F32), ((bins, width), F32),
@@ -547,7 +622,7 @@
             in_specs=[
                 pl.BlockSpec((1, feature, cells), lambda i, s: (s[i], 0, 0)),
                 pl.BlockSpec(memory_space=pltpu.SMEM),
-                pl.BlockSpec((2, per // 2, bins, rows), lambda i, s: (0, i, 0, 0)),
+                pl.BlockSpec((1, 2, per // 2, bins, rows), lambda i, s: (i // deep, 0, lax.rem(i, deep), 0, 0)),
                 pl.BlockSpec((per, bins, rows), lambda i, s: (i, 0, 0)),
                 const(sums.shape),
             ],

time: 307 us -> 264 us (0.86)
  the two profiles are of different devices: /device:TPU:15 before, /device:TPU:60 now
where the time goes in v2:
time: 264 us
  Pallas kernels  257 us (97%)
  local copies, waits for them, and re-layouts  3.37 us (1%)
    pallas_call x1, Pallas kernels, give_back(): pl.pallas_call(functools.partial(return_kernel, row_devs, col_devs, scale...  102 us
    pallas_call x1, Pallas kernels, exchange(): pl.pallas_call(functools.partial(exchange_kernel, row_devs, col_devs), na...  76.4 us
    pallas_call x1, Pallas kernels, compute(): pl.pallas_call(functools.partial(compute_kernel, cols, rows), name='pair_...  67 us
    pallas_call x1, Pallas kernels, finish(): pl.pallas_call(functools.partial(finish_kernel, hidden), name='finish', g...  11.7 us

profile of v2, /device:TPU:60, one launch (start us, length us, event | category | flops | bytes accessed | tf_op | source)
XLA Modules:
  0.0 263.5 jit_solution(3092344587262014814)
XLA Ops:
  0.6 0.7 convert_divide_fusion.inv_ref
  1.3 0.0 copy-start.1
  1.3 0.9 convert_reduce_fusion
  2.2 0.7 multiply_add_fusion
  2.9 0.0 copy-start
  2.9 0.1 select_reduce_fusion.1
  3.0 0.1 select_reduce_fusion
  3.1 0.1 sub.7
  3.2 0.7 reshape.52.inv_ref
  3.9 0.7 reshape.51.idx_ref
  4.6 0.6 broadcast_in_dim.20.ids_ref
  5.2 76.4 %exchange.1 = (bf16[16,2,64,1024]{3,2,1,0:T(8,128)(2,1)}, s32[16,8,128]{2,1,0:T(8,128)}, bf16[4,2,8,64,128]{4,3,2,1,0:T(8,128)(2,1)}) custom-call(s32[16,2]{1,0:T(8,128)} %reshape.51.idx_ref, f32[16,2]{1,0:T(8,128)} %reshape.52.inv_ref, s32[16,8,128]{2,1,0:T(8,128)} %broadcast_in_dim.20.ids_ref, bf16[16,64,1024]{2,1,0:T(8,128)(2,1)} %bitcast.20, ...), custom_call_target="tpu_custom_call" | custom-call | tf_op jit(solution)/shard_map/exchange/pallas_call | solution.py:236
  81.6 67.0 %pair_block.1 = (f32[128,64,128]{2,1,0:T(8,128)}, bf16[8,64,1024]{2,1,0:T(8,128)(2,1)}, bf16[64,64,128]{2,1,0:T(8,128)(2,1)}, bf16[64,64,128]{2,1,0:T(8,128)(2,1)}, f32[2048,128]{1,0:T(8,128)}) custom-call(s32[16,8,128]{2,1,0:T(8,128)} %get-tuple-element.29.ids_ref, f32[128,64,128]{2,1,0:T(8,128)} %pair_ref.1, ...), custom_call_target="tpu_custom_call" | custom-call | tf_op jit(solution)/shard_map/pair_block/pallas_call | solution.py:396
  148.6 0.0 copy-done.1
  148.6 0.0 copy-done
  148.6 101.9 %give_back.1 = (bf16[16,2,64,1024]{3,2,1,0:T(8,128)(2,1)}, bf16[4,2,8,64,128]{4,3,2,1,0:T(8,128)(2,1)}, bf16[8,16,16,128]{3,2,1,0:T(8,128)(2,1)}) custom-call(s32[16,8,128]{2,1,0:T(8,128)} %get-tuple-element.29.ids_ref, bf16[8,64,1024]{2,1,0:T(8,128)(2,1)} %get-tuple-element.32.g_ref, bf16[2,4,8,64,128]{4,3,2,1,0:T(8,128)(2,1)} %bitcast.21, ...), custom_call_target="tpu_custom_call" | custom-call | tf_op jit(solution)/shard_map/give_back/pallas_call | solution.py:545
  250.5 11.7 %finish.1 = (bf16[16,64,1024]{2,1,0:T(8,128)(2,1)}, bf16[64,64,128]{2,1,0:T(8,128)(2,1)}, f32[64,128]{1,0:T(8,128)}, f32[128,512]{1,0:T(8,128)}, f32[128,512]{1,...) custom-call(s32[16]{0:T(128)} %copy-done, bf16[32,64,1024]{2,1,0:T(8,128)(2,1)} %bitcast.17, ...), custom_call_target="tpu_custom_call" | custom-call | tf_op jit(solution)/shard_map/finish/pallas_call | solution.py:616
  262.3 1.3 slice_bitcast_fusion
  (2 shorter events, 0.0 us)
Async XLA Ops:
  1.3 147.3 %copy-start.1 = (f32[16]{0:T(128)}, f32[16]{0:T(128)S(1)}, u32[]{:S(2)}) copy-start(f32[16]{0:T(128)S(1)} %convert_divide_fusion.inv_ref) | copy-start | bytes 196
  2.9 145.7 %copy-start = (s32[16]{0:T(128)}, s32[16]{0:T(128)S(1)}, u32[]{:S(2)}) copy-start(s32[16]{0:T(128)S(1)} %get-tuple-element.52.slot_ref) | copy-start | bytes 196

commit v3 on v2

v3 whole, which is shorter than its diff:
```python
import functools

import jax
import jax.numpy as jnp
from jax import lax
from jax.experimental import pallas as pl
from jax.experimental.pallas import tpu as pltpu
from jax.sharding import PartitionSpec as P

SQ = 32
CAP = 2
MESH = pl.DeviceIdType.MESH
F32 = jnp.float32
BF16 = jnp.bfloat16
ROWS_SUM = 2048
VMEM_LIMIT = 60 * 1024 * 1024


def vmem():
    return pl.BlockSpec(memory_space=pltpu.VMEM)


def smem():
    return pl.BlockSpec(memory_space=pltpu.SMEM)


def hbm():
    return pl.BlockSpec(memory_space=pl.ANY)


def nn(a, b):
    return lax.dot_general(a, b, (((1,), (0,)), ((), ())), preferred_element_type=F32)


def nt(a, b):
    return lax.dot_general(a, b, (((1,), (1,)), ((), ())), preferred_element_type=F32)


def tn(a, b):
    return lax.dot_general(a, b, (((0,), (0,)), ((), ())), preferred_element_type=F32)


def displacements(col_devs):
    if col_devs != 16:
        return (1, col_devs), [(0, k) for k in range(1, col_devs)]
    order = [(0, 1), (1, 0), (0, 3), (3, 0), (1, 1), (3, 3), (1, 3), (3, 1),
             (0, 2), (2, 0), (1, 2), (2, 1), (3, 2), (2, 3), (2, 2)]
    return (4, 4), order


def moved(col, shape, step, sign):
    ys, zs = shape
    y = lax.rem(col // zs + sign * step[0] + ys, ys)
    z = lax.rem(lax.rem(col, zs) + sign * step[1] + zs, zs)
    return y * zs + z


class Place:
    def __init__(self, row_devs, col_devs):
        self.row, self.col = lax.axis_index("row"), lax.axis_index("col")
        self.xs, self.zs = row_devs // 2, col_devs // (row_devs // 2)
        self.x, self.k = self.row // 2, lax.rem(self.row, 2)
        self.y, self.z = self.col // self.zs, lax.rem(self.col, self.zs)

    def turn(self, value, by):
        return lax.rem(value + by, self.xs) if self.xs > 1 else value


class Mirror:
    def __init__(self, place, src, first, second, dst, sems):
        self.p, self.src, self.first, self.second, self.dst = place, src, first, second, dst
        self.s1, self.r1, self.s2, self.r2, self.s3, self.r3, self.own = sems

    def along_x(self, source, target, send, recv):
        p = self.p
        copies = []
        for n in range(1, p.xs):
            to = p.turn(p.x, n)
            copies.append(pltpu.make_async_remote_copy(
                src_ref=source(to), dst_ref=target.at[p.x], send_sem=send.at[n - 1], recv_sem=recv.at[n - 1],
                device_id=(2 * to + p.k, p.col), device_id_type=MESH))
        return copies

    def start_1(self):
        p = self.p
        self.copies = self.along_x(lambda to: self.src.at[:, to], self.first, self.s1, self.r1)
        for copy in self.copies:
            copy.start()
        self.local = pltpu.make_async_copy(self.src.at[:, p.x], self.first.at[p.x], self.own.at[0])
        self.local.start()

    def finish(self):
        self.local.wait()
        for copy in self.copies:
            copy.wait()

    finish_1 = finish_3 = finish

    def start_2(self):
        p = self.p
        self.plan = []
        for n in range(p.xs):
            to_y = p.turn(p.y, n)
            for h in (0, 1):
                to_z, to_k = 2 * p.k + h, p.z // 2
                source, target = self.first.at[to_y, h], self.second.at[p.y, lax.rem(p.z, 2)]
                slot = 2 * n + lax.rem(p.z, 2)
                remote = pltpu.make_async_remote_copy(
                    src_ref=source, dst_ref=target, send_sem=self.s2.at[2 * n + h], recv_sem=self.r2.at[slot],
                    device_id=(2 * p.x + to_k, to_y * p.zs + to_z), device_id_type=MESH)
                if n == 0:
                    here = jnp.logical_and(to_k == p.k, to_z == p.z)
                    local = pltpu.make_async_copy(source, target, self.r2.at[slot])
                    start_one(here, remote, local)
                    self.plan.append((here, remote))
                else:
                    remote.start()
                    self.plan.append((None, remote))

    def finish_2(self):
        for i, (here, remote) in enumerate(self.plan):
            if here is None:
                remote.wait_send()
            else:
                @pl.when(jnp.logical_not(here))
                def _():
                    remote.wait_send()
            ref = self.second.at[0, 0]
            pltpu.make_async_copy(ref, ref, self.r2.at[i]).wait()

    def start_3(self):
        p = self.p
        self.copies = self.along_x(lambda to: self.second.at[to], self.dst, self.s3, self.r3)
        for copy in self.copies:
            copy.start()
        self.local = pltpu.make_async_copy(self.second.at[p.x], self.dst.at[p.x], self.own.at[1])
        self.local.start()


def start_one(here, remote, local):
    @pl.when(jnp.logical_not(here))
    def _():
        remote.start()

    @pl.when(here)
    def _():
        local.start()


def mirror_sems(row_devs):
    xs = row_devs // 2
    dma = lambda n: pltpu.SemaphoreType.DMA((n,))
    return [dma(max(xs - 1, 1)), dma(max(xs - 1, 1)), dma(2 * xs), dma(2 * xs),
            dma(max(xs - 1, 1)), dma(max(xs - 1, 1)), dma(2)]


def greet(p, row_devs, col_devs):
    barrier = pltpu.get_barrier_semaphore()
    peers = 0
    for n in range(1, col_devs):
        pl.semaphore_signal(barrier, inc=1, device_id=(p.row, lax.rem(p.col + n, col_devs)), device_id_type=MESH)
        peers += 1
    for n in range(1, row_devs):
        pl.semaphore_signal(barrier, inc=1, device_id=(lax.rem(p.row + n, row_devs), p.col), device_id_type=MESH)
        peers += 1
    for n in range(1, col_devs):
        pl.semaphore_signal(
            barrier, inc=1, device_id=(2 * p.x + 1 - p.k, lax.rem(p.col + n, col_devs)), device_id_type=MESH)
        peers += 1
    return lambda: pl.semaphore_wait(barrier, peers)


BAND = 8
CHUNKS = SQ // BAND
SPAN = BAND * SQ
PART = 256


def window_kernel(row_devs, col_devs, scale, idx_ref, inv_ref, ids_ref, tiles_ref, cot_ref, pair_ref, wt_ref,
                  gain_ref, bias_ref, wg_ref, wu_ref, wo_ref, wd_ref,
                  back_ref, heads_ref, sum_ref, gp_ref, hl_ref, got_ref,
                  sendbuf, recv, names, onehot, s_ref, g_ref, pair_v, d_ref, z_ref, hs_ref,
                  pack, c_first, c_second, c_dst, h_first, h_second,
                  ag_ref, au_ref, ao_ref, ad_ref, at_ref, an_ref, acc_ref,
                  low, rs_recv, cs_send, cs_recv, piece, chunk,
                  pair_sem, out_sem, id_send, id_recv, t_send, t_recv, g_send, g_recv, own_t, own_g, own_sem,
                  a_send, a_recv, b_send, b_recv, e_send, e_recv, f_send, f_recv, *mirror_sem):
    p = Place(row_devs, col_devs)
    row, col = p.row, p.col
    shape, order = displacements(col_devs)
    rows, cols, width = pair_v.shape
    bins, feature, hidden = wd_ref.shape[0], wt_ref.shape[0], wg_ref.shape[1]
    sq_cols, sq_rows = cols // SQ, rows // SQ
    squares = sq_cols * sq_rows
    cells = BAND * cols
    greeted = greet(p, row_devs, col_devs)
    pair_in = pltpu.make_async_copy(pair_ref, pair_v, pair_sem.at[0])
    pair_in.start()

    lanes = rows
    left = lax.broadcasted_iota(jnp.int32, (bins, lanes), 1) < lanes // 2

    def pack_pair(n, carry):
        u, v = cot_ref[2 * n].astype(F32), cot_ref[2 * n + 1].astype(F32)
        m, t = n // pack.shape[2], lax.rem(n, pack.shape[2])
        pack[0, m, t] = jnp.where(left, u, pltpu.roll(v, lanes // 2, 1)).astype(BF16)
        pack[1, m, t] = jnp.where(left, pltpu.roll(u, lanes // 2, 1), v).astype(BF16)
        return carry

    lax.fori_loop(0, cols // 2, pack_pair, 0)

    def fill(d, carry):
        for k in range(CAP):
            tile = (tiles_ref[idx_ref[d, k]].astype(F32) * inv_ref[d, k]).astype(BF16)
            for q in range(CHUNKS):
                sendbuf[q, d, k] = tile[:, q * SPAN:(q + 1) * SPAN]
        return carry

    lax.fori_loop(0, col_devs, fill, 0)
    greeted()

    mirror = Mirror(p, pack, c_first, c_second, c_dst, mirror_sem[:7])
    mirror.start_1()

    def to_all(source, target, send, recv_sem):
        copies = []
        for n, step in enumerate(order):
            to = moved(col, shape, step, 1)
            copies.append(pltpu.make_async_remote_copy(
                src_ref=source(to), dst_ref=target(n), send_sem=send(n), recv_sem=recv_sem(n),
                device_id=(row, to), device_id_type=MESH))
        return copies

    def local(source, target, sem):
        copy = pltpu.make_async_copy(source, target, sem)
        copy.start()
        return copy

    id_copies = to_all(lambda to: ids_ref.at[to], lambda n: got_ref.at[col],
                       lambda n: id_send.at[n], lambda n: id_recv.at[n])
    for copy in id_copies:
        copy.start()
    own_id = local(ids_ref.at[col], got_ref.at[col], own_sem.at[0])
    tile_copies = []
    for q in range(CHUNKS):
        tile_copies.append(to_all(lambda to: sendbuf.at[q, to], lambda n: recv.at[q, col],
                                  lambda n: t_send.at[q, n], lambda n: t_recv.at[q, n]))
    own_tiles = [local(sendbuf.at[q, col], recv.at[q, col], own_t.at[q]) for q in range(CHUNKS)]
    for copy in tile_copies[0]:
        copy.start()

    for ref in (ag_ref, au_ref, ao_ref, ad_ref, at_ref, an_ref):
        ref[...] = jnp.zeros(ref.shape, F32)
    mirror.finish()
    mirror.start_2()
    for q in range(1, CHUNKS):
        for copy in tile_copies[q]:
            copy.start()

    def own_cot(j, carry):
        d_ref[pl.ds(j, rows, stride=cols), :] = cot_ref[j].astype(F32).T
        return carry

    lax.fori_loop(0, cols, own_cot, 0)
    own_id.wait()
    for copy in id_copies:
        copy.wait()
    to_smem = local(got_ref, names, own_sem.at[1])
    to_smem.wait()
    one_rows = lax.broadcasted_iota(jnp.int32, (squares * feature, CAP * feature), 0)
    one_cols = lax.broadcasted_iota(jnp.int32, (squares * feature, CAP * feature), 1)
    same = lax.rem(one_rows, feature) == lax.rem(one_cols, feature)
    square_of = one_rows // feature
    for d in range(col_devs):
        wanted = jnp.where(one_cols < feature, names[d, 0, 0], names[d, 0, 1])
        onehot[:, d * CAP * feature:(d + 1) * CAP * feature] = jnp.where(
            jnp.logical_and(same, square_of == wanted), 1.0, 0.0).astype(BF16)
    mirror.finish_2()
    mirror.start_3()
    mirror.finish()

    def mirrored(n, carry):
        at = pl.multiple_of(n * rows, rows)
        d_ref[pl.ds(at, rows), :] += c_dst[
            lax.rem(n, cols // 2) // c_dst.shape[2], n // (cols // 2), lax.rem(n, c_dst.shape[2])].astype(F32).T
        return carry

    lax.fori_loop(0, cols, mirrored, 0)
    pair_in.wait()

    def band(q, a, carry):
        row0 = a * SQ + q * BAND
        w_t = wt_ref[...]
        pieces = [s_ref[a * sq_cols + d] for d in range(sq_cols)]
        proj = jnp.concatenate(
            [tn(one, w_t).reshape(BAND, SQ, width) for one in pieces], axis=1).reshape(cells, width)
        z1 = pair_v[pl.ds(row0, BAND)].reshape(cells, width) + proj
        gain, bias = gain_ref[...], bias_ref[...]
        mean = jnp.mean(z1, axis=1, keepdims=True)
        centered = z1 - mean
        rdev = lax.rsqrt(jnp.mean(centered * centered, axis=1, keepdims=True) + 1e-5)
        xhat = centered * rdev
        normed = (xhat * gain + bias).astype(BF16)
        base = pl.multiple_of(row0 * cols, cells)
        dheads = d_ref[pl.ds(base, cells), :].astype(BF16)
        wd = wd_ref[...]
        dz2 = nn(dheads, wd)
        dzl = dz2.astype(BF16)
        normed_t = normed.T
        dzl_t = dzl.T
        z2 = z1
        dnorm = jnp.zeros((cells, width), F32)
        for k in range(hidden // PART):
            span = slice(k * PART, (k + 1) * PART)
            gate = nn(normed, wg_ref[:, span])
            up = nn(normed, wu_ref[:, span])
            dhid = nt(dzl, wo_ref[span, :])
            s = 0.5 * jnp.tanh(0.5 * gate) + 0.5
            swish = gate * s
            hid = (swish * up).astype(BF16)
            dup = (dhid * swish).astype(BF16)
            dgate = (dhid * up * (s + swish * (1.0 - s))).astype(BF16)
            z2 = z2 + nn(hid, wo_ref[span, :])
            dnorm = dnorm + nt(dgate, wg_ref[:, span]) + nt(dup, wu_ref[:, span])
            ao_ref[:, span] += nn(dzl_t, hid)
            ag_ref[:, span] += nn(normed_t, dgate)
            au_ref[:, span] += nn(normed_t, dup)
        z_ref[pl.ds(base, cells), :] = z2
        z2_low = z2.astype(BF16)
        heads_t = nt(wd, z2_low).astype(BF16)
        pairs = BAND // 2
        deep = pairs // p.xs
        for u in range(pairs):
            t = (q % 2 * 2 + lax.rem(a, 2)) * deep + u // p.xs
            hs_ref[q // 2, a // 2, u % p.xs, t] = heads_t[:, u * 128:(u + 1) * 128]
        ad_ref[...] += tn(dheads, z2_low)
        an_ref[0] += jnp.sum((dnorm * xhat).reshape(cells // 8, 8, width), axis=0)
        an_ref[1] += jnp.sum(dnorm.reshape(cells // 8, 8, width), axis=0)
        dx = dnorm * gain
        grad = dz2 + (dx - jnp.mean(dx, axis=1, keepdims=True)
                      - xhat * jnp.mean(dx * xhat, axis=1, keepdims=True)) * rdev
        grad3 = grad.reshape(BAND, cols, width)
        pair_v[pl.ds(row0, BAND)] = grad3
        total = jnp.zeros((feature, width), F32)
        for d in range(sq_cols):
            dproj = grad3[:, d * SQ:(d + 1) * SQ, :].reshape(SPAN, width).astype(BF16)
            g_ref[a * sq_cols + d] = nt(w_t, dproj).astype(BF16)
            total = total + nn(pieces[d], dproj)
        at_ref[...] += total
        return carry

    back_copies, own_back, pair_out = [], [], []
    halves = [Mirror(p, hs_ref.at[n], h_first.at[n], h_second.at[n], heads_ref.at[n],
                     mirror_sem[7 * (n + 1):7 * (n + 2)]) for n in range(2)]
    for q in range(CHUNKS):
        own_tiles[q].wait()
        for copy in tile_copies[q]:
            copy.wait()
        s_ref[...] = nn(onehot[...], recv[q].reshape(col_devs * CAP * feature, SPAN)).astype(BF16).reshape(
            s_ref.shape)
        lax.fori_loop(0, sq_rows, functools.partial(band, q), 0)

        def take(d, carry):
            for k in range(CAP):
                sendbuf[q, d, k] = g_ref[jnp.maximum(names[d, 0, k], 0)]
            return carry

        lax.fori_loop(0, col_devs, take, 0)
        for a in range(sq_rows):
            part_rows = pl.ds(a * SQ + q * BAND, BAND)
            pair_out.append(local(pair_v.at[part_rows], gp_ref.at[part_rows], out_sem.at[q * sq_rows + a]))
        if q == 1:
            halves[0].start_1()
        if q == 2:
            halves[0].finish()
            halves[0].start_2()
        if q == 3:
            halves[0].finish_2()
            halves[0].start_3()
            halves[1].start_1()
        back_copies.append(to_all(lambda to: sendbuf.at[q, to], lambda n: back_ref.at[q, col],
                                  lambda n: g_send.at[q, n], lambda n: g_recv.at[q, n]))
        own_back.append(local(sendbuf.at[q, col], back_ref.at[q, col], own_g.at[q]))
        if q < CHUNKS - 1:
            for copy in back_copies[q]:
                copy.start()

    for k in range(hidden // width):
        span = slice(k * width, (k + 1) * width)
        acc_ref[k * width:(k + 1) * width, :] = ag_ref[:, span]
        acc_ref[hidden + k * width:hidden + (k + 1) * width, :] = au_ref[:, span]
        acc_ref[2 * hidden + k * width:2 * hidden + (k + 1) * width, :] = ao_ref[:, span].T
    tail = 3 * hidden
    acc_ref[tail:tail + bins, :] = ad_ref[...]
    tail += bins
    acc_ref[tail:tail + feature, :] = at_ref[...]
    tail += feature
    acc_ref[tail:tail + 8, :] = an_ref[0]
    acc_ref[tail + 8:tail + 16, :] = an_ref[1]
    acc_ref[tail + 16:, :] = jnp.zeros((ROWS_SUM - tail - 16, width), F32)
    low[...] = acc_ref[...].astype(BF16)
    rows_chunk = ROWS_SUM // row_devs

    def part(r):
        return pl.ds(pl.multiple_of(r * rows_chunk, rows_chunk), rows_chunk)

    first = []
    for k in range(1, row_devs):
        to = lax.rem(row + k, row_devs)
        first.append(pltpu.make_async_remote_copy(
            src_ref=low.at[part(to)], dst_ref=rs_recv.at[k - 1], send_sem=a_send.at[k - 1],
            recv_sem=a_recv.at[k - 1], device_id=(to, col), device_id_type=MESH))
    for copy in first:
        copy.start()
    bulk = back_copies[-1]
    third = (len(bulk) + 2) // 3
    for copy in bulk[:third]:
        copy.start()

    wd = wd_ref[...]

    def local_heads(j, carry):
        zj = z_ref[pl.ds(j, rows, stride=cols), :].astype(BF16)
        hl_ref[j] = nt(wd, zj).astype(BF16)
        return carry

    lax.fori_loop(0, cols, local_heads, 0)
    halves[1].finish_1()
    halves[1].start_2()
    for copy in first:
        copy.wait()
    total = acc_ref[part(row), :]
    for k in range(row_devs - 1):
        total = total + rs_recv[k].astype(F32)
    cs_send[...] = total.astype(BF16).reshape(cs_send.shape)
    second = to_all(lambda to: cs_send.at[to], lambda n: cs_recv.at[n],
                    lambda n: b_send.at[n], lambda n: b_recv.at[n])
    for copy in second:
        copy.start()
    for copy in bulk[third:2 * third]:
        copy.start()
    for copy in second:
        copy.wait()
    mine = cs_send[col].astype(F32)
    for k in range(col_devs - 1):
        mine = mine + cs_recv[k].astype(F32)
    piece[...] = (mine * scale).astype(BF16)
    chunk[col] = piece[...]
    gather = to_all(lambda to: piece, lambda n: chunk.at[col], lambda n: e_send.at[n], lambda n: e_recv.at[n])
    for copy in gather:
        copy.start()
    for copy in bulk[2 * third:]:
        copy.start()
    halves[1].finish_2()
    halves[1].start_3()
    for copy in gather:
        copy.wait()
    last = []
    for k in range(1, row_devs):
        last.append(pltpu.make_async_remote_copy(
            src_ref=chunk, dst_ref=sum_ref.at[row], send_sem=f_send.at[k - 1],
            recv_sem=f_recv.at[k - 1], device_id=(lax.rem(row + k, row_devs), col), device_id_type=MESH))
    for copy in last:
        copy.start()
    local(chunk, sum_ref.at[row], own_sem.at[2]).wait()
    for copy in pair_out:
        copy.wait()
    halves[0].finish_3()
    for copy in last:
        copy.wait()
    halves[1].finish_3()
    for q in range(CHUNKS):
        own_back[q].wait()
        for copy in back_copies[q]:
            copy.wait()


def window(row_devs, col_devs, scale, idx, inv, ids, tiles_t, cot_t, pair, *weights):
    slots, feature, cells_sq = tiles_t.shape
    cols, bins, rows = cot_t.shape
    width = pair.shape[2]
    hidden = weights[3].shape[1]
    squares = rows // SQ * (cols // SQ)
    peers, xs = col_devs - 1, row_devs // 2
    rows_chunk = ROWS_SUM // row_devs
    rows_piece = rows_chunk // col_devs
    dma = lambda *n: pltpu.SemaphoreType.DMA(n)
    slices = (2, xs, cols // 2 // xs, bins, rows)
    cot_slices = (xs, 2) + slices[2:]
    head_deep = cols // 4 // xs
    heads = (2, xs, 2, head_deep, bins, 128)
    return pl.pallas_call(
        functools.partial(window_kernel, row_devs, col_devs, scale),
        name="window",
        out_shape=(
            jax.ShapeDtypeStruct((CHUNKS, col_devs, CAP, feature, SPAN), BF16),
            jax.ShapeDtypeStruct(heads, BF16),
            jax.ShapeDtypeStruct((row_devs, col_devs, rows_piece, 128), BF16),
            jax.ShapeDtypeStruct(pair.shape, F32),
            jax.ShapeDtypeStruct((cols, bins, rows), BF16),
            jax.ShapeDtypeStruct((col_devs, 8, 128), jnp.int32),
        ),
        in_specs=[smem(), smem(), vmem(), vmem(), vmem(), hbm()] + [vmem()] * len(weights),
        out_specs=(hbm(), hbm(), hbm(), hbm(), vmem(), hbm()),
        scratch_shapes=[
            pltpu.VMEM((CHUNKS, col_devs, CAP, feature, SPAN), BF16),
            pltpu.VMEM((CHUNKS, col_devs, CAP, feature, SPAN), BF16),
            pltpu.SMEM((col_devs, 8, 128), jnp.int32),
            pltpu.VMEM((squares * feature, col_devs * CAP * feature), BF16),
            pltpu.VMEM((squares, feature, SPAN), BF16),
            pltpu.VMEM((squares, feature, SPAN), BF16),
            pltpu.VMEM((rows, cols, width), F32),
            pltpu.VMEM((rows * cols, bins), F32),
            pltpu.VMEM((rows * cols, width), F32),
            pltpu.VMEM((2, 2, xs, head_deep, bins, 128), BF16),
            pltpu.VMEM(slices, BF16),
            pltpu.VMEM(cot_slices, BF16),
            pltpu.VMEM(cot_slices, BF16),
            pltpu.VMEM(cot_slices, BF16),
            pltpu.VMEM(heads, BF16),
            pltpu.VMEM(heads, BF16),
            pltpu.VMEM((width, hidden), F32),
            pltpu.VMEM((width, hidden), F32),
            pltpu.VMEM((width, hidden), F32),
            pltpu.VMEM((bins, width), F32),
            pltpu.VMEM((feature, width), F32),
            pltpu.VMEM((2, 8, width), F32),
            pltpu.VMEM((ROWS_SUM, 128), F32),
            pltpu.VMEM((ROWS_SUM, 128), BF16),
            pltpu.VMEM((row_devs - 1, rows_chunk, 128), BF16),
            pltpu.VMEM((col_devs, rows_piece, 128), BF16),
            pltpu.VMEM((col_devs - 1, rows_piece, 128), BF16),
            pltpu.VMEM((rows_piece, 128), BF16),
            pltpu.VMEM((col_devs, rows_piece, 128), BF16),
            dma(1), dma(rows // BAND), dma(peers), dma(peers),
            dma(CHUNKS, peers), dma(CHUNKS, peers), dma(CHUNKS, peers), dma(CHUNKS, peers),
            dma(CHUNKS), dma(CHUNKS), dma(3),
            dma(row_devs - 1), dma(row_devs - 1), dma(peers), dma(peers),
            dma(peers), dma(peers), dma(row_devs - 1), dma(row_devs - 1),
        ] + mirror_sems(row_devs) * 3,
        compiler_params=pltpu.CompilerParams(
            collective_id=0, has_side_effects=True, vmem_limit_bytes=VMEM_LIMIT),
    )(idx, inv, ids, tiles_t, cot_t, pair, *weights)


def finish_kernel(hidden, slot_ref, back_ref, inv_ref, mir_ref, hl_ref, sum_ref,
                  tile_ref, log_ref, gt_ref, gg_ref, gu_ref, go_ref, gd_ref, gn_ref):
    step = pl.program_id(0)
    span = back_ref.shape[3]
    for q in range(back_ref.shape[0]):
        tile_ref[0, :, q * span:(q + 1) * span] = (back_ref[q, 0].astype(F32) * inv_ref[step]).astype(BF16)
    per, bins, lanes = hl_ref.shape
    xs = mir_ref.shape[1]
    pairs = BAND // 2
    low = lax.broadcasted_iota(jnp.int32, (bins, lanes), 1) < lanes // 2
    for k in range(per // 2):
        n = step * (per // 2) + k
        u, q, a = lax.rem(n, pairs), lax.rem(n // pairs, CHUNKS), n // (pairs * CHUNKS)
        m, t = lax.rem(u, xs), (lax.rem(q, 2) * 2 + a) * (pairs // xs) + u // xs
        a, b = mir_ref[q // 2, m, 0, t].astype(F32), mir_ref[q // 2, m, 1, t].astype(F32)
        even = jnp.where(low, a, pltpu.roll(b, lanes // 2, 1))
        odd = jnp.where(low, pltpu.roll(a, lanes // 2, 1), b)
        log_ref[2 * k] = (hl_ref[2 * k].astype(F32) + even).astype(BF16)
        log_ref[2 * k + 1] = (hl_ref[2 * k + 1].astype(F32) + odd).astype(BF16)

    @pl.when(step == 0)
    def _():
        width = sum_ref.shape[1]
        for k in range(hidden // width):
            span = slice(k * width, (k + 1) * width)
            gg_ref[:, span] = sum_ref[k * width:(k + 1) * width, :].astype(F32)
            gu_ref[:, span] = sum_ref[hidden + k * width:hidden + (k + 1) * width, :].astype(F32)
        go_ref[...] = sum_ref[2 * hidden:3 * hidden, :].astype(F32)
        at = 3 * hidden
        gd_ref[...] = sum_ref[at:at + gd_ref.shape[0], :].astype(F32)
        at += gd_ref.shape[0]
        gt_ref[...] = sum_ref[at:at + gt_ref.shape[0], :].astype(F32)
        at += gt_ref.shape[0]
        norm = sum_ref[at:at + 16, :].astype(F32)
        gn_ref[0:1, :] = jnp.sum(norm[0:8], axis=0, keepdims=True)
        gn_ref[1:2, :] = jnp.sum(norm[8:16], axis=0, keepdims=True)


def finish(hidden, slot_of, inv, back, mir, hl, sums):
    slots = slot_of.shape[0]
    feature, cells = back.shape[2], back.shape[0] * back.shape[3]
    cols, bins, rows = hl.shape
    width = sums.shape[1]
    per = cols // slots
    const = lambda shape: pl.BlockSpec(shape, lambda i, s: (0,) * len(shape))
    outs = [((slots, feature, cells), BF16), ((cols, bins, rows), BF16), ((feature, width), F32),
            ((width, hidden), F32), ((width, hidden), F32), ((hidden, width), F32), ((bins, width), F32),
            ((2, width), F32)]
    return pl.pallas_call(
        functools.partial(finish_kernel, hidden),
        name="finish",
        grid_spec=pltpu.PrefetchScalarGridSpec(
            num_scalar_prefetch=1,
            grid=(slots,),
            in_specs=[
                pl.BlockSpec((back.shape[0], 1, feature, back.shape[3]), lambda i, s: (0, s[i], 0, 0)),
                pl.BlockSpec(memory_space=pltpu.SMEM),
                const(mir.shape),
                pl.BlockSpec((per, bins, rows), lambda i, s: (i, 0, 0)),
                const(sums.shape),
            ],
            out_specs=[
                pl.BlockSpec((1, feature, cells), lambda i, s: (i, 0, 0)),
                pl.BlockSpec((per, bins, rows), lambda i, s: (i, 0, 0)),
            ] + [const(shape) for shape, _ in outs[2:]],
        ),
        out_shape=[jax.ShapeDtypeStruct(shape, kind) for shape, kind in outs],
        compiler_params=pltpu.CompilerParams(
            dimension_semantics=("arbitrary",), vmem_limit_bytes=VMEM_LIMIT),
    )(slot_of, back, inv, mir, hl, sums)


def per_device(pair, logit_cotangent, tiles, tile_target, tile_square, tile_count, w_template,
               transition_norm_gain, transition_norm_bias, w_gate, w_up, w_out, w_dist):
    row_devs = lax.axis_size("row")
    col_devs = lax.axis_size("col")
    rows, cols, width = pair.shape
    length = rows * row_devs
    slots, cells_sq, feature = tiles.shape
    hidden = w_gate.shape[1]
    tiles_t = jnp.transpose(tiles, (0, 2, 1))
    cot_t = jnp.transpose(logit_cotangent, (1, 2, 0))
    target = tile_target[:, 0]
    places = jnp.arange(slots, dtype=jnp.int32)
    rank = jnp.sum((target[:, None] == target[None, :]) & (places[None, :] < places[:, None]),
                   axis=1, dtype=jnp.int32)
    slot_of = target * CAP + rank
    inv_count = 1.0 / tile_count.astype(F32)
    chosen = slot_of[None, :] == jnp.arange(col_devs * CAP, dtype=jnp.int32)[:, None]
    picked = chosen.astype(jnp.int32)
    idx = jnp.sum(picked * places[None, :], axis=1).reshape(col_devs, CAP)
    send_inv = jnp.sum(jnp.where(chosen, inv_count[None, :], 0.0), axis=1).reshape(col_devs, CAP)
    send_ids = (jnp.sum(picked * (tile_square + 1)[None, :], axis=1) - 1).reshape(col_devs, CAP)
    ids = jnp.broadcast_to(jnp.pad(send_ids, ((0, 0), (0, 128 - CAP)))[:, None, :], (col_devs, 8, 128))

    back, mir_heads, sums, grad_pair, hl, _ = window(
        row_devs, col_devs, 1.0 / length, idx, send_inv, ids, tiles_t, cot_t, pair, w_template,
        transition_norm_gain[None, :], transition_norm_bias[None, :], w_gate, w_up, w_out, w_dist.T)
    grad_tiles_t, logits_t, g_template, g_gate, g_up, g_out, g_dist_t, g_norm = finish(
        hidden, slot_of, inv_count, back.reshape(CHUNKS, col_devs * CAP, feature, SPAN), mir_heads, hl,
        sums.reshape(ROWS_SUM, width))
    return (
        jnp.transpose(logits_t, (2, 0, 1)),
        grad_pair,
        jnp.transpose(grad_tiles_t, (0, 2, 1)),
        g_template,
        g_norm[0],
        g_norm[1],
        g_gate,
        g_up,
        g_out,
        g_dist_t.T,
    )


def solution(mesh):
    return jax.shard_map(
        per_device,
        mesh=mesh,
        in_specs=(
            P("row", "col", None),
            P("row", "col", None),
            P(("row", "col"), None, None),
            P(("row", "col"), None),
            P(("row", "col")),
            P(("row", "col")),
            P(), P(), P(), P(), P(), P(), P(),
        ),
        out_specs=(
            P("row", "col", None),
            P("row", "col", None),
            P(("row", "col"), None, None),
            P(), P(), P(), P(), P(), P(), P(),
        ),
        check_vma=False,
    )
```

time: 264 us -> 179 us (0.68)
  the two profiles are of different devices: /device:TPU:60 before, /device:TPU:1 now
where the time goes in v3:
time: 179 us; the launch traced here: 178 us
  Pallas kernels  167 us (93%)
  local copies, waits for them, and re-layouts  8.17 us (5%)
  other arithmetic  2.43 us (1%)
    pallas_call x1, Pallas kernels, window(): pl.pallas_call(functools.partial(window_kernel, row_devs, col_devs, scale...  155 us
    pallas_call x1, Pallas kernels, finish(): pl.pallas_call(functools.partial(finish_kernel, hidden), name='finish', g...  12 us
    unnamed x5, local copies, waits for them, and re-layouts  4.79 us

profile of v3, /device:TPU:1, one launch (start us, length us, event | category | flops | bytes accessed | tf_op | source)
XLA Modules:
  0.0 178.4 jit_solution(3835075433694216088)
XLA Ops:
  0.6 0.7 convert_divide_fusion.inv_ref
  1.3 0.0 copy-start.1
  1.3 0.9 convert_reduce_fusion
  2.2 0.7 multiply_add_fusion
  2.9 0.0 copy-start
  2.9 0.1 select_reduce_fusion.1
  3.0 0.1 select_reduce_fusion
  3.1 0.1 sub.7
  3.2 0.7 reshape.49.inv_ref
  3.9 0.7 reshape.48.idx_ref
  4.6 0.6 broadcast_in_dim.20.ids_ref
  5.2 155.1 %window.1 = (bf16[4,16,2,64,256]{4,3,2,1,0:T(8,128)(2,1)}, bf16[2,4,2,4,64,128]{5,4,3,2,1,0:T(8,128)(2,1)}, bf16[8,16,16,128]{3,2,1,0:T(8,128)(2,1)}, f32[128,64...) custom-call(s32[16,2]{1,0:T(8,128)} %reshape.48.idx_ref, f32[16,2]{1,0:T(8,128)} %reshape.49.inv_ref, ...), custom_call_target="tpu_custom_call" | custom-call | tf_op jit(solution)/shard_map/window/pallas_call | solution.py:492
  160.3 0.0 copy-done.1
  160.3 0.0 copy-done
  160.3 12.0 %finish.1 = (bf16[16,64,1024]{2,1,0:T(8,128)(2,1)}, bf16[64,64,128]{2,1,0:T(8,128)(2,1)}, f32[64,128]{1,0:T(8,128)}, f32[128,512]{1,0:T(8,128)}, f32[128,512]{1,...) custom-call(s32[16]{0:T(128)} %copy-done, bf16[4,32,64,256]{3,2,1,0:T(8,128)(2,1)} %bitcast.16, ...), custom_call_target="tpu_custom_call" | custom-call | tf_op jit(solution)/shard_map/finish/pallas_call | solution.py:594
  172.3 1.3 slice_bitcast_fusion
  173.6 4.8 %copy.24 = f32[128,64,128]{2,1,0:T(8,128)} copy(f32[128,64,128]{2,1,0:T(8,128)} %get-tuple-element.53) | data formatting | bytes 8388608
  (2 shorter events, 0.0 us)
Async XLA Ops:
  1.3 159.0 %copy-start.1 = (f32[16]{0:T(128)}, f32[16]{0:T(128)S(1)}, u32[]{:S(2)}) copy-start(f32[16]{0:T(128)S(1)} %convert_divide_fusion.inv_ref) | copy-start | bytes 196
  2.9 157.4 %copy-start = (s32[16]{0:T(128)}, s32[16]{0:T(128)S(1)}, u32[]{:S(2)}) copy-start(s32[16]{0:T(128)S(1)} %get-tuple-element.40.slot_ref) | copy-start | bytes 196

commit v4 on v3

--- a/solution.py
+++ b/solution.py
@@ -176,10 +176,20 @@
 PART = 256
 
 
-def window_kernel(row_devs, col_devs, scale, idx_ref, inv_ref, ids_ref, tiles_ref, cot_ref, pair_ref, wt_ref,
+def share(count):
+    inv = jnp.where(count == 1, 1.0, jnp.where(count == 2, 0.5, jnp.where(count == 3, 1.0 / 3.0, 0.25)))
+    return jnp.where(count == 0, 0.0, inv).astype(F32)
+
+
+def pair_place(n, xs):
+    u, q, a = lax.rem(n, BAND // 2), lax.rem(n // (BAND // 2), CHUNKS), n // (BAND // 2 * CHUNKS)
+    return q // 2, lax.rem(u, xs), (lax.rem(q, 2) * 2 + a) * (BAND // 2 // xs) + u // xs
+
+
+def window_kernel(row_devs, col_devs, scale, code_ref, tiles_ref, cot_ref, pair_ref, wt_ref,
                   gain_ref, bias_ref, wg_ref, wu_ref, wo_ref, wd_ref,
                   back_ref, heads_ref, sum_ref, gp_ref, hl_ref, got_ref,
-                  sendbuf, recv, names, onehot, s_ref, g_ref, pair_v, d_ref, z_ref, hs_ref,
+                  ids_ref, sendbuf, recv, names, onehot, s_ref, g_ref, pair_v, d_ref, z_ref, hs_ref,
                   pack, c_first, c_second, c_dst, h_first, h_second,
                   ag_ref, au_ref, ao_ref, ad_ref, at_ref, an_ref, acc_ref,
                   low, rs_recv, cs_send, cs_recv, piece, chunk,
@@ -202,25 +212,31 @@
 
     def pack_pair(n, carry):
         u, v = cot_ref[2 * n].astype(F32), cot_ref[2 * n + 1].astype(F32)
-        m, t = n // pack.shape[2], lax.rem(n, pack.shape[2])
-        pack[0, m, t] = jnp.where(left, u, pltpu.roll(v, lanes // 2, 1)).astype(BF16)
-        pack[1, m, t] = jnp.where(left, pltpu.roll(u, lanes // 2, 1), v).astype(BF16)
+        half, m, t = pair_place(n, p.xs)
+        pack[half, 0, m, t] = jnp.where(left, u, pltpu.roll(v, lanes // 2, 1)).astype(BF16)
+        pack[half, 1, m, t] = jnp.where(left, pltpu.roll(u, lanes // 2, 1), v).astype(BF16)
         return carry
 
     lax.fori_loop(0, cols // 2, pack_pair, 0)
 
-    def fill(d, carry):
+    def fill(parts, d, carry):
         for k in range(CAP):
-            tile = (tiles_ref[idx_ref[d, k]].astype(F32) * inv_ref[d, k]).astype(BF16)
-            for q in range(CHUNKS):
-                sendbuf[q, d, k] = tile[:, q * SPAN:(q + 1) * SPAN]
+            code = code_ref[d, k]
+            at, inv = jnp.bitwise_and(code, 255), share(code // 65536)
+            for q in parts:
+                sendbuf[q, d, k] = (
+                    tiles_ref[at, :, q * SPAN:(q + 1) * SPAN].astype(F32) * inv).astype(BF16)
         return carry
 
-    lax.fori_loop(0, col_devs, fill, 0)
+    lax.fori_loop(0, col_devs, functools.partial(fill, (0,)), 0)
+    id_lane = lax.broadcasted_iota(jnp.int32, (8, 128), 1)
+    for d in range(col_devs):
+        ids_ref[d] = jnp.where(id_lane == 0, code_ref[d, 0], code_ref[d, 1])
     greeted()
 
-    mirror = Mirror(p, pack, c_first, c_second, c_dst, mirror_sem[:7])
-    mirror.start_1()
+    mirrors = [Mirror(p, pack.at[n], c_first.at[n], c_second.at[n], c_dst.at[n], mirror_sem[7 * n:7 * (n + 1)])
+               for n in range(2)]
+    mirrors[0].start_1()
 
     def to_all(source, target, send, recv_sem):
         copies = []
@@ -245,17 +261,18 @@
     for q in range(CHUNKS):
         tile_copies.append(to_all(lambda to: sendbuf.at[q, to], lambda n: recv.at[q, col],
                                   lambda n: t_send.at[q, n], lambda n: t_recv.at[q, n]))
+    ahead = len(order) // 2
+    for copy in tile_copies[0][:ahead]:
+        copy.start()
+    mirrors[1].start_1()
+    lax.fori_loop(0, col_devs, functools.partial(fill, tuple(range(1, CHUNKS))), 0)
     own_tiles = [local(sendbuf.at[q, col], recv.at[q, col], own_t.at[q]) for q in range(CHUNKS)]
-    for copy in tile_copies[0]:
-        copy.start()
-
     for ref in (ag_ref, au_ref, ao_ref, ad_ref, at_ref, an_ref):
         ref[...] = jnp.zeros(ref.shape, F32)
-    mirror.finish()
-    mirror.start_2()
-    for q in range(1, CHUNKS):
-        for copy in tile_copies[q]:
-            copy.start()
+    mirrors[0].finish_1()
+    mirrors[0].start_2()
+    for copy in tile_copies[0][ahead:] + tile_copies[1]:
+        copy.start()
 
     def own_cot(j, carry):
         d_ref[pl.ds(j, rows, stride=cols), :] = cot_ref[j].astype(F32).T
@@ -265,27 +282,36 @@
     own_id.wait()
     for copy in id_copies:
         copy.wait()
-    to_smem = local(got_ref, names, own_sem.at[1])
-    to_smem.wait()
+    local(got_ref, names, own_sem.at[1]).wait()
+
+    def square(d, k):
+        return jnp.bitwise_and(names[d, 0, k] // 256, 255) - 1
+
     one_rows = lax.broadcasted_iota(jnp.int32, (squares * feature, CAP * feature), 0)
     one_cols = lax.broadcasted_iota(jnp.int32, (squares * feature, CAP * feature), 1)
     same = lax.rem(one_rows, feature) == lax.rem(one_cols, feature)
     square_of = one_rows // feature
     for d in range(col_devs):
-        wanted = jnp.where(one_cols < feature, names[d, 0, 0], names[d, 0, 1])
+        wanted = jnp.where(one_cols < feature, square(d, 0), square(d, 1))
         onehot[:, d * CAP * feature:(d + 1) * CAP * feature] = jnp.where(
             jnp.logical_and(same, square_of == wanted), 1.0, 0.0).astype(BF16)
-    mirror.finish_2()
-    mirror.start_3()
-    mirror.finish()
-
-    def mirrored(n, carry):
-        at = pl.multiple_of(n * rows, rows)
-        d_ref[pl.ds(at, rows), :] += c_dst[
-            lax.rem(n, cols // 2) // c_dst.shape[2], n // (cols // 2), lax.rem(n, c_dst.shape[2])].astype(F32).T
+    mirrors[1].finish_1()
+    mirrors[1].start_2()
+    for copy in tile_copies[2] + tile_copies[3]:
+        copy.start()
+    mirrors[0].finish_2()
+    mirrors[0].start_3()
+
+    def mirrored(half, r, carry):
+        parity, r = r // (cols // 4), lax.rem(r, cols // 4)
+        n = r // BAND * (2 * BAND) + half * BAND + lax.rem(r, BAND)
+        _, m, t = pair_place(n, p.xs)
+        at = pl.multiple_of((parity * (cols // 2) + n) * rows, rows)
+        d_ref[pl.ds(at, rows), :] += c_dst[half, m, parity, t].astype(F32).T
         return carry
 
-    lax.fori_loop(0, cols, mirrored, 0)
+    mirrors[0].finish_3()
+    lax.fori_loop(0, cols // 2, functools.partial(mirrored, 0), 0)
     pair_in.wait()
 
     def band(q, a, carry):
@@ -351,8 +377,11 @@
 
     back_copies, own_back, pair_out = [], [], []
     halves = [Mirror(p, hs_ref.at[n], h_first.at[n], h_second.at[n], heads_ref.at[n],
-                     mirror_sem[7 * (n + 1):7 * (n + 2)]) for n in range(2)]
+                     mirror_sem[7 * (n + 2):7 * (n + 3)]) for n in range(2)]
     for q in range(CHUNKS):
+        if q == 2:
+            mirrors[1].finish_3()
+            lax.fori_loop(0, cols // 2, functools.partial(mirrored, 1), 0)
         own_tiles[q].wait()
         for copy in tile_copies[q]:
             copy.wait()
@@ -362,13 +391,16 @@
 
         def take(d, carry):
             for k in range(CAP):
-                sendbuf[q, d, k] = g_ref[jnp.maximum(names[d, 0, k], 0)]
+                sendbuf[q, d, k] = g_ref[jnp.maximum(square(d, k), 0)]
             return carry
 
         lax.fori_loop(0, col_devs, take, 0)
         for a in range(sq_rows):
             part_rows = pl.ds(a * SQ + q * BAND, BAND)
             pair_out.append(local(pair_v.at[part_rows], gp_ref.at[part_rows], out_sem.at[q * sq_rows + a]))
+        if q == 0:
+            mirrors[1].finish_2()
+            mirrors[1].start_3()
         if q == 1:
             halves[0].start_1()
         if q == 2:
@@ -414,8 +446,6 @@
         copy.start()
     bulk = back_copies[-1]
     third = (len(bulk) + 2) // 3
-    for copy in bulk[:third]:
-        copy.start()
 
     wd = wd_ref[...]
 
@@ -437,7 +467,7 @@
                     lambda n: b_send.at[n], lambda n: b_recv.at[n])
     for copy in second:
         copy.start()
-    for copy in bulk[third:2 * third]:
+    for copy in bulk[:2 * third]:
         copy.start()
     for copy in second:
         copy.wait()
@@ -475,7 +505,7 @@
             copy.wait()
 
 
-def window(row_devs, col_devs, scale, idx, inv, ids, tiles_t, cot_t, pair, *weights):
+def window(row_devs, col_devs, scale, code, tiles_t, cot_t, pair, *weights):
     slots, feature, cells_sq = tiles_t.shape
     cols, bins, rows = cot_t.shape
     width = pair.shape[2]
@@ -485,10 +515,9 @@
     rows_chunk = ROWS_SUM // row_devs
     rows_piece = rows_chunk // col_devs
     dma = lambda *n: pltpu.SemaphoreType.DMA(n)
-    slices = (2, xs, cols // 2 // xs, bins, rows)
-    cot_slices = (xs, 2) + slices[2:]
-    head_deep = cols // 4 // xs
-    heads = (2, xs, 2, head_deep, bins, 128)
+    deep = cols // 4 // xs
+    slices = (2, 2, xs, deep, bins, rows)
+    heads = (2, xs, 2, deep, bins, rows)
     return pl.pallas_call(
         functools.partial(window_kernel, row_devs, col_devs, scale),
         name="window",
@@ -500,9 +529,10 @@
             jax.ShapeDtypeStruct((cols, bins, rows), BF16),
             jax.ShapeDtypeStruct((col_devs, 8, 128), jnp.int32),
         ),
-        in_specs=[smem(), smem(), vmem(), vmem(), vmem(), hbm()] + [vmem()] * len(weights),
+        in_specs=[smem(), vmem(), vmem(), hbm()] + [vmem()] * len(weights),
         out_specs=(hbm(), hbm(), hbm(), hbm(), vmem(), hbm()),
         scratch_shapes=[
+            pltpu.VMEM((col_devs, 8, 128), jnp.int32),
             pltpu.VMEM((CHUNKS, col_devs, CAP, feature, SPAN), BF16),
             pltpu.VMEM((CHUNKS, col_devs, CAP, feature, SPAN), BF16),
             pltpu.SMEM((col_devs, 8, 128), jnp.int32),
@@ -512,11 +542,11 @@
             pltpu.VMEM((rows, cols, width), F32),
             pltpu.VMEM((rows * cols, bins), F32),
             pltpu.VMEM((rows * cols, width), F32),
-            pltpu.VMEM((2, 2, xs, head_deep, bins, 128), BF16),
             pltpu.VMEM(slices, BF16),
-            pltpu.VMEM(cot_slices, BF16),
-            pltpu.VMEM(cot_slices, BF16),
-            pltpu.VMEM(cot_slices, BF16),
+            pltpu.VMEM(slices, BF16),
+            pltpu.VMEM(heads, BF16),
+            pltpu.VMEM(heads, BF16),
+            pltpu.VMEM(heads, BF16),
             pltpu.VMEM(heads, BF16),
             pltpu.VMEM(heads, BF16),
             pltpu.VMEM((width, hidden), F32),
@@ -537,27 +567,32 @@
             dma(CHUNKS), dma(CHUNKS), dma(3),
             dma(row_devs - 1), dma(row_devs - 1), dma(peers), dma(peers),
             dma(peers), dma(peers), dma(row_devs - 1), dma(row_devs - 1),
-        ] + mirror_sems(row_devs) * 3,
+        ] + mirror_sems(row_devs) * 4,
         compiler_params=pltpu.CompilerParams(
             collective_id=0, has_side_effects=True, vmem_limit_bytes=VMEM_LIMIT),
-    )(idx, inv, ids, tiles_t, cot_t, pair, *weights)
-
-
-def finish_kernel(hidden, slot_ref, back_ref, inv_ref, mir_ref, hl_ref, sum_ref,
-                  tile_ref, log_ref, gt_ref, gg_ref, gu_ref, go_ref, gd_ref, gn_ref):
+    )(code, tiles_t, cot_t, pair, *weights)
+
+
+STEPS = 4
+
+
+def finish_kernel(hidden, slot_ref, *refs):
+    each = slot_ref.shape[0] // STEPS
+    backs, refs = refs[:each], refs[each:]
+    (count_ref, mir_ref, hl_ref, sum_ref, gp_ref,
+     tile_ref, log_ref, out_ref, gt_ref, gg_ref, gu_ref, go_ref, gd_ref, gn_ref) = refs
     step = pl.program_id(0)
-    span = back_ref.shape[3]
-    for q in range(back_ref.shape[0]):
-        tile_ref[0, :, q * span:(q + 1) * span] = (back_ref[q, 0].astype(F32) * inv_ref[step]).astype(BF16)
+    out_ref[...] = gp_ref[...]
+    for n, back_ref in enumerate(backs):
+        inv = share(count_ref[step * each + n])
+        span = back_ref.shape[3]
+        for q in range(back_ref.shape[0]):
+            tile_ref[n, :, q * span:(q + 1) * span] = (back_ref[q, 0].astype(F32) * inv).astype(BF16)
     per, bins, lanes = hl_ref.shape
-    xs = mir_ref.shape[1]
-    pairs = BAND // 2
     low = lax.broadcasted_iota(jnp.int32, (bins, lanes), 1) < lanes // 2
     for k in range(per // 2):
-        n = step * (per // 2) + k
-        u, q, a = lax.rem(n, pairs), lax.rem(n // pairs, CHUNKS), n // (pairs * CHUNKS)
-        m, t = lax.rem(u, xs), (lax.rem(q, 2) * 2 + a) * (pairs // xs) + u // xs
-        a, b = mir_ref[q // 2, m, 0, t].astype(F32), mir_ref[q // 2, m, 1, t].astype(F32)
+        half, m, t = pair_place(step * (per // 2) + k, mir_ref.shape[1])
+        a, b = mir_ref[half, m, 0, t].astype(F32), mir_ref[half, m, 1, t].astype(F32)
         even = jnp.where(low, a, pltpu.roll(b, lanes // 2, 1))
         odd = jnp.where(low, pltpu.roll(a, lanes // 2, 1), b)
         log_ref[2 * k] = (hl_ref[2 * k].astype(F32) + even).astype(BF16)
@@ -581,38 +616,42 @@
         gn_ref[1:2, :] = jnp.sum(norm[8:16], axis=0, keepdims=True)
 
 
-def finish(hidden, slot_of, inv, back, mir, hl, sums):
+def finish(hidden, slot_of, count, back, mir, hl, sums, grad_pair):
     slots = slot_of.shape[0]
     feature, cells = back.shape[2], back.shape[0] * back.shape[3]
     cols, bins, rows = hl.shape
     width = sums.shape[1]
-    per = cols // slots
+    per, each = cols // STEPS, slots // STEPS
     const = lambda shape: pl.BlockSpec(shape, lambda i, s: (0,) * len(shape))
-    outs = [((slots, feature, cells), BF16), ((cols, bins, rows), BF16), ((feature, width), F32),
-            ((width, hidden), F32), ((width, hidden), F32), ((hidden, width), F32), ((bins, width), F32),
-            ((2, width), F32)]
+    outs = [((slots, feature, cells), BF16), ((cols, bins, rows), BF16), (grad_pair.shape, F32),
+            ((feature, width), F32), ((width, hidden), F32), ((width, hidden), F32), ((hidden, width), F32),
+            ((bins, width), F32), ((2, width), F32)]
+    held = lambda n: pl.BlockSpec(
+        (back.shape[0], 1, feature, back.shape[3]), lambda i, s: (0, s[i * each + n], 0, 0))
+    band = pl.BlockSpec((grad_pair.shape[0] // STEPS,) + grad_pair.shape[1:], lambda i, s: (i, 0, 0))
     return pl.pallas_call(
         functools.partial(finish_kernel, hidden),
         name="finish",
         grid_spec=pltpu.PrefetchScalarGridSpec(
             num_scalar_prefetch=1,
-            grid=(slots,),
-            in_specs=[
-                pl.BlockSpec((back.shape[0], 1, feature, back.shape[3]), lambda i, s: (0, s[i], 0, 0)),
+            grid=(STEPS,),
+            in_specs=[held(n) for n in range(each)] + [
                 pl.BlockSpec(memory_space=pltpu.SMEM),
                 const(mir.shape),
                 pl.BlockSpec((per, bins, rows), lambda i, s: (i, 0, 0)),
                 const(sums.shape),
+                band,
             ],
             out_specs=[
-                pl.BlockSpec((1, feature, cells), lambda i, s: (i, 0, 0)),
+                pl.BlockSpec((each, feature, cells), lambda i, s: (i, 0, 0)),
                 pl.BlockSpec((per, bins, rows), lambda i, s: (i, 0, 0)),
-            ] + [const(shape) for shape, _ in outs[2:]],
+                band,
+            ] + [const(shape) for shape, _ in outs[3:]],
         ),
         out_shape=[jax.ShapeDtypeStruct(shape, kind) for shape, kind in outs],
         compiler_params=pltpu.CompilerParams(
             dimension_semantics=("arbitrary",), vmem_limit_bytes=VMEM_LIMIT),
-    )(slot_of, back, inv, mir, hl, sums)
+    )(slot_of, *([back] * each), count, mir, hl, sums, grad_pair)
 
 
 def per_device(pair, logit_cotangent, tiles, tile_target, tile_square, tile_count, w_template,
@@ -630,20 +669,16 @@
     rank = jnp.sum((target[:, None] == target[None, :]) & (places[None, :] < places[:, None]),
                    axis=1, dtype=jnp.int32)
     slot_of = target * CAP + rank
-    inv_count = 1.0 / tile_count.astype(F32)
     chosen = slot_of[None, :] == jnp.arange(col_devs * CAP, dtype=jnp.int32)[:, None]
-    picked = chosen.astype(jnp.int32)
-    idx = jnp.sum(picked * places[None, :], axis=1).reshape(col_devs, CAP)
-    send_inv = jnp.sum(jnp.where(chosen, inv_count[None, :], 0.0), axis=1).reshape(col_devs, CAP)
-    send_ids = (jnp.sum(picked * (tile_square + 1)[None, :], axis=1) - 1).reshape(col_devs, CAP)
-    ids = jnp.broadcast_to(jnp.pad(send_ids, ((0, 0), (0, 128 - CAP)))[:, None, :], (col_devs, 8, 128))
-
-    back, mir_heads, sums, grad_pair, hl, _ = window(
-        row_devs, col_devs, 1.0 / length, idx, send_inv, ids, tiles_t, cot_t, pair, w_template,
+    label = places + 256 * (tile_square + 1) + 65536 * tile_count
+    code = jnp.sum(jnp.where(chosen, label[None, :], 0), axis=1).reshape(col_devs, CAP)
+
+    back, mir_heads, sums, gp, hl, _ = window(
+        row_devs, col_devs, 1.0 / length, code, tiles_t, cot_t, pair, w_template,
         transition_norm_gain[None, :], transition_norm_bias[None, :], w_gate, w_up, w_out, w_dist.T)
-    grad_tiles_t, logits_t, g_template, g_gate, g_up, g_out, g_dist_t, g_norm = finish(
-        hidden, slot_of, inv_count, back.reshape(CHUNKS, col_devs * CAP, feature, SPAN), mir_heads, hl,
-        sums.reshape(ROWS_SUM, width))
+    grad_tiles_t, logits_t, grad_pair, g_template, g_gate, g_up, g_out, g_dist_t, g_norm = finish(
+        hidden, slot_of, tile_count, back.reshape(CHUNKS, col_devs * CAP, feature, SPAN), mir_heads, hl,
+        sums.reshape(ROWS_SUM, width), gp)
     return (
         jnp.transpose(logits_t, (2, 0, 1)),
         grad_pair,

time: 179 us -> 175 us (0.978)
  local copies, waits for them, and re-layouts: 8.17 us -> 1.91 us
  Pallas kernels: 167 us -> 170 us
    pallas_call x1, Pallas kernels: 155 us -> 162 us  [window(): pl.pallas_call(functools.partial(window_kernel, row_devs, col_devs, scale...]
    unnamed x5 -> x2, local copies, waits for them, and re-layouts: 4.79 us -> 0.01 us
    pallas_call x1, Pallas kernels: 12 us -> 8.48 us  [finish(): pl.pallas_call(functools.partial(finish_kernel, hidden), name='finish', g...]
where the time goes in v4:
time: 175 us; the launch traced here: 174 us
  Pallas kernels  170 us (97%)
  local copies, waits for them, and re-layouts  1.91 us (1%)
    pallas_call x1, Pallas kernels, window(): pl.pallas_call(functools.partial(window_kernel, row_devs, col_devs, scale...  162 us
    pallas_call x1, Pallas kernels, finish(): pl.pallas_call(functools.partial(finish_kernel, hidden), name='finish', g...  8.48 us

profile of v4, /device:TPU:1, one launch (start us, length us, event | category | flops | bytes accessed | tf_op | source)
XLA Modules:
  0.0 174.3 jit_solution(10675341698926148157)
XLA Ops:
  0.6 0.9 convert_reduce_fusion
  1.6 0.7 multiply_add_fusion
  2.3 0.0 copy-start
  2.3 0.1 select_reduce_fusion
  2.3 0.7 reshape.39.code_ref
  3.0 161.6 %window.1 = (bf16[4,16,2,64,256]{4,3,2,1,0:T(8,128)(2,1)}, bf16[2,4,2,4,64,128]{5,4,3,2,1,0:T(8,128)(2,1)}, bf16[8,16,16,128]{3,2,1,0:T(8,128)(2,1)}, f32[128,64...) custom-call(s32[16,2]{1,0:T(8,128)} %reshape.39.code_ref, bf16[16,64,1024]{2,1,0:T(8,128)(2,1)} %bitcast.20, ...), custom_call_target="tpu_custom_call" | custom-call | tf_op jit(solution)/shard_map/window/pallas_call | solution.py:521
  164.6 0.0 copy-done
  164.6 8.5 %finish.1 = (bf16[16,64,1024]{2,1,0:T(8,128)(2,1)}, bf16[64,64,128]{2,1,0:T(8,128)(2,1)}, f32[128,64,128]{2,1,0:T(8,128)}, f32[64,128]{1,0:T(8,128)}, f32[128,51...) custom-call(s32[16]{0:T(128)} %copy-done, ...), custom_call_target="tpu_custom_call" | custom-call | tf_op jit(solution)/shard_map/finish/pallas_call | solution.py:632
  173.1 1.2 slice_bitcast_fusion
Async XLA Ops:
  2.3 162.4 %copy-start = (s32[16]{0:T(128)}, s32[16]{0:T(128)S(1)}, u32[]{:S(2)}) copy-start(s32[16]{0:T(128)S(1)} %get-tuple-element.41.slot_ref) | copy-start | bytes 196

commit v5 on v4

--- a/solution.py
+++ b/solution.py
@@ -217,8 +217,6 @@
         pack[half, 1, m, t] = jnp.where(left, pltpu.roll(u, lanes // 2, 1), v).astype(BF16)
         return carry
 
-    lax.fori_loop(0, cols // 2, pack_pair, 0)
-
     def fill(parts, d, carry):
         for k in range(CAP):
             code = code_ref[d, k]
@@ -234,10 +232,6 @@
         ids_ref[d] = jnp.where(id_lane == 0, code_ref[d, 0], code_ref[d, 1])
     greeted()
 
-    mirrors = [Mirror(p, pack.at[n], c_first.at[n], c_second.at[n], c_dst.at[n], mirror_sem[7 * n:7 * (n + 1)])
-               for n in range(2)]
-    mirrors[0].start_1()
-
     def to_all(source, target, send, recv_sem):
         copies = []
         for n, step in enumerate(order):
@@ -261,9 +255,12 @@
     for q in range(CHUNKS):
         tile_copies.append(to_all(lambda to: sendbuf.at[q, to], lambda n: recv.at[q, col],
                                   lambda n: t_send.at[q, n], lambda n: t_recv.at[q, n]))
-    ahead = len(order) // 2
-    for copy in tile_copies[0][:ahead]:
-        copy.start()
+    for copy in tile_copies[0]:
+        copy.start()
+    lax.fori_loop(0, cols // 2, pack_pair, 0)
+    mirrors = [Mirror(p, pack.at[n], c_first.at[n], c_second.at[n], c_dst.at[n], mirror_sem[7 * n:7 * (n + 1)])
+               for n in range(2)]
+    mirrors[0].start_1()
     mirrors[1].start_1()
     lax.fori_loop(0, col_devs, functools.partial(fill, tuple(range(1, CHUNKS))), 0)
     own_tiles = [local(sendbuf.at[q, col], recv.at[q, col], own_t.at[q]) for q in range(CHUNKS)]
@@ -271,7 +268,7 @@
         ref[...] = jnp.zeros(ref.shape, F32)
     mirrors[0].finish_1()
     mirrors[0].start_2()
-    for copy in tile_copies[0][ahead:] + tile_copies[1]:
+    for copy in tile_copies[1]:
         copy.start()
 
     def own_cot(j, carry):
@@ -407,13 +404,11 @@
             halves[0].finish()
             halves[0].start_2()
         if q == 3:
-            halves[0].finish_2()
-            halves[0].start_3()
             halves[1].start_1()
         back_copies.append(to_all(lambda to: sendbuf.at[q, to], lambda n: back_ref.at[q, col],
                                   lambda n: g_send.at[q, n], lambda n: g_recv.at[q, n]))
         own_back.append(local(sendbuf.at[q, col], back_ref.at[q, col], own_g.at[q]))
-        if q < CHUNKS - 1:
+        if q < CHUNKS - 2:
             for copy in back_copies[q]:
                 copy.start()
 
@@ -444,8 +439,8 @@
             recv_sem=a_recv.at[k - 1], device_id=(to, col), device_id_type=MESH))
     for copy in first:
         copy.start()
-    bulk = back_copies[-1]
-    third = (len(bulk) + 2) // 3
+    held = back_copies[2] + back_copies[3]
+    some = len(order) // 3
 
     wd = wd_ref[...]
 
@@ -467,8 +462,10 @@
                     lambda n: b_send.at[n], lambda n: b_recv.at[n])
     for copy in second:
         copy.start()
-    for copy in bulk[:2 * third]:
-        copy.start()
+    for copy in held[:some]:
+        copy.start()
+    halves[0].finish_2()
+    halves[0].start_3()
     for copy in second:
         copy.wait()
     mine = cs_send[col].astype(F32)
@@ -479,7 +476,7 @@
     gather = to_all(lambda to: piece, lambda n: chunk.at[col], lambda n: e_send.at[n], lambda n: e_recv.at[n])
     for copy in gather:
         copy.start()
-    for copy in bulk[2 * third:]:
+    for copy in held[some:]:
         copy.start()
     halves[1].finish_2()
     halves[1].start_3()

time: 175 us -> 152 us (0.87); the launches traced: 174 us -> 149 us
  Pallas kernels: 170 us -> 145 us
    pallas_call x1, Pallas kernels: 162 us -> 137 us  [window(): pl.pallas_call(functools.partial(window_kernel, row_devs, col_devs, scale...]
where the time goes in v5:
time: 152 us; the launch traced here: 149 us
  Pallas kernels  145 us (95%)
  local copies, waits for them, and re-layouts  1.91 us (1%)
  other arithmetic  1.7 us (1%)
    pallas_call x1, Pallas kernels, window(): pl.pallas_call(functools.partial(window_kernel, row_devs, col_devs, scale...  137 us
    pallas_call x1, Pallas kernels, finish(): pl.pallas_call(functools.partial(finish_kernel, hidden), name='finish', g...  8.48 us

profile of v5, /device:TPU:1, one launch (start us, length us, event | category | flops | bytes accessed | tf_op | source)
XLA Modules:
  0.0 149.3 jit_solution(17233827121230354010)
XLA Ops:
  0.6 0.9 convert_reduce_fusion
  1.6 0.7 multiply_add_fusion
  2.3 0.0 copy-start
  2.3 0.1 select_reduce_fusion
  2.3 0.7 reshape.39.code_ref
  3.0 136.5 %window.1 = (bf16[4,16,2,64,256]{4,3,2,1,0:T(8,128)(2,1)}, bf16[2,4,2,4,64,128]{5,4,3,2,1,0:T(8,128)(2,1)}, bf16[8,16,16,128]{3,2,1,0:T(8,128)(2,1)}, f32[128,64...) custom-call(s32[16,2]{1,0:T(8,128)} %reshape.39.code_ref, bf16[16,64,1024]{2,1,0:T(8,128)(2,1)} %bitcast.20, ...), custom_call_target="tpu_custom_call" | custom-call | tf_op jit(solution)/shard_map/window/pallas_call | solution.py:518
  139.5 0.0 copy-done
  139.6 8.5 %finish.1 = (bf16[16,64,1024]{2,1,0:T(8,128)(2,1)}, bf16[64,64,128]{2,1,0:T(8,128)(2,1)}, f32[128,64,128]{2,1,0:T(8,128)}, f32[64,128]{1,0:T(8,128)}, f32[128,51...) custom-call(s32[16]{0:T(128)} %copy-done, ...), custom_call_target="tpu_custom_call" | custom-call | tf_op jit(solution)/shard_map/finish/pallas_call | solution.py:629
  148.0 1.2 slice_bitcast_fusion
Async XLA Ops:
  2.3 137.3 %copy-start = (s32[16]{0:T(128)}, s32[16]{0:T(128)S(1)}, u32[]{:S(2)}) copy-start(s32[16]{0:T(128)S(1)} %get-tuple-element.41.slot_ref) | copy-start | bytes 196

commit v6 on v5

--- a/solution.py
+++ b/solution.py
@@ -174,6 +174,7 @@
 CHUNKS = SQ // BAND
 SPAN = BAND * SQ
 PART = 256
+EARLY, MIDDLE = 7, 5
 
 
 def share(count):
@@ -388,7 +389,8 @@
 
         def take(d, carry):
             for k in range(CAP):
-                sendbuf[q, d, k] = g_ref[jnp.maximum(square(d, k), 0)]
+                inv = share(names[d, 0, k] // 65536)
+                sendbuf[q, d, k] = (g_ref[jnp.maximum(square(d, k), 0)].astype(F32) * inv).astype(BF16)
             return carry
 
         lax.fori_loop(0, col_devs, take, 0)
@@ -408,8 +410,8 @@
         back_copies.append(to_all(lambda to: sendbuf.at[q, to], lambda n: back_ref.at[q, col],
                                   lambda n: g_send.at[q, n], lambda n: g_recv.at[q, n]))
         own_back.append(local(sendbuf.at[q, col], back_ref.at[q, col], own_g.at[q]))
-        if q < CHUNKS - 2:
-            for copy in back_copies[q]:
+        if q < CHUNKS - 1:
+            for copy in back_copies[q] if q < CHUNKS - 2 else back_copies[q][:EARLY]:
                 copy.start()
 
     for k in range(hidden // width):
@@ -439,8 +441,7 @@
             recv_sem=a_recv.at[k - 1], device_id=(to, col), device_id_type=MESH))
     for copy in first:
         copy.start()
-    held = back_copies[2] + back_copies[3]
-    some = len(order) // 3
+    held = back_copies[2][EARLY:] + back_copies[3]
 
     wd = wd_ref[...]
 
@@ -462,7 +463,7 @@
                     lambda n: b_send.at[n], lambda n: b_recv.at[n])
     for copy in second:
         copy.start()
-    for copy in held[:some]:
+    for copy in held[:MIDDLE]:
         copy.start()
     halves[0].finish_2()
     halves[0].start_3()
@@ -476,7 +477,7 @@
     gather = to_all(lambda to: piece, lambda n: chunk.at[col], lambda n: e_send.at[n], lambda n: e_recv.at[n])
     for copy in gather:
         copy.start()
-    for copy in held[some:]:
+    for copy in held[MIDDLE:]:
         copy.start()
     halves[1].finish_2()
     halves[1].start_3()
@@ -566,89 +567,109 @@
             dma(peers), dma(peers), dma(row_devs - 1), dma(row_devs - 1),
         ] + mirror_sems(row_devs) * 4,
         compiler_params=pltpu.CompilerParams(
-            collective_id=0, has_side_effects=True, vmem_limit_bytes=VMEM_LIMIT),
+            collective_id=0, has_side_effects=True, vmem_limit_bytes=42 * 1024 * 1024),
     )(code, tiles_t, cot_t, pair, *weights)
 
 
 STEPS = 4
 
 
-def finish_kernel(hidden, slot_ref, *refs):
-    each = slot_ref.shape[0] // STEPS
-    backs, refs = refs[:each], refs[each:]
-    (count_ref, mir_ref, hl_ref, sum_ref, gp_ref,
-     tile_ref, log_ref, out_ref, gt_ref, gg_ref, gu_ref, go_ref, gd_ref, gn_ref) = refs
-    step = pl.program_id(0)
-    out_ref[...] = gp_ref[...]
-    for n, back_ref in enumerate(backs):
-        inv = share(count_ref[step * each + n])
-        span = back_ref.shape[3]
-        for q in range(back_ref.shape[0]):
-            tile_ref[n, :, q * span:(q + 1) * span] = (back_ref[q, 0].astype(F32) * inv).astype(BF16)
-    per, bins, lanes = hl_ref.shape
+def finish_kernel(hidden, slot_ref, back_ref, mir_ref, hl_ref, sum_ref, gp_ref,
+                  tile_ref, log_ref, out_ref, gt_ref, gg_ref, gu_ref, go_ref, gd_ref, gn_ref, gb_ref,
+                  mir, local, total, gp, tile, back_sem, in_sem, gp_in, gp_out, tile_sem, log_sem):
+    slots = tile.shape[0]
+    cols, bins, lanes = local.shape
+    width = total.shape[1]
+
+    def begin(source, target, sem):
+        copy = pltpu.make_async_copy(source, target, sem)
+        copy.start()
+        return copy
+
+    deep = gp.shape[0] // STEPS
+    bands = [pl.ds(n * deep, deep) for n in range(STEPS)]
+    pair_in = [begin(gp_ref.at[bands[0]], gp.at[bands[0]], gp_in.at[0])]
+    get_sum = begin(sum_ref, total, in_sem.at[0])
+    span = back_ref.shape[3]
+    tiles_in = [[begin(back_ref.at[q, slot_ref[n]], tile.at[n, :, pl.ds(q * span, span)], back_sem.at[n, q])
+                 for q in range(CHUNKS)] for n in range(slots)]
+    get_mir = begin(mir_ref, mir, in_sem.at[1])
+    get_local = begin(hl_ref, local, in_sem.at[2])
+    pair_in += [begin(gp_ref.at[bands[n]], gp.at[bands[n]], gp_in.at[n]) for n in range(1, STEPS)]
+    leaving = []
+    pair_in[0].wait()
+    leaving.append(begin(gp.at[bands[0]], out_ref.at[bands[0]], gp_out.at[0]))
+
+    get_sum.wait()
+    for k in range(hidden // width):
+        span = slice(k * width, (k + 1) * width)
+        gg_ref[:, span] = total[k * width:(k + 1) * width, :].astype(F32)
+        gu_ref[:, span] = total[hidden + k * width:hidden + (k + 1) * width, :].astype(F32)
+    go_ref[...] = total[2 * hidden:3 * hidden, :].astype(F32)
+    at = 3 * hidden
+    gd_ref[...] = total[at:at + gd_ref.shape[0], :].astype(F32)
+    at += gd_ref.shape[0]
+    gt_ref[...] = total[at:at + gt_ref.shape[0], :].astype(F32)
+    at += gt_ref.shape[0]
+    norm = total[at:at + 16, :].astype(F32)
+    gn_ref[...] = jnp.sum(norm[0:8], axis=0, keepdims=True)
+    gb_ref[...] = jnp.sum(norm[8:16], axis=0, keepdims=True)
+
+    for n in range(slots):
+        for copy in tiles_in[n]:
+            copy.wait()
+        leaving.append(begin(tile.at[n], tile_ref.at[n], tile_sem.at[n]))
+
+    get_mir.wait()
+    get_local.wait()
     low = lax.broadcasted_iota(jnp.int32, (bins, lanes), 1) < lanes // 2
-    for k in range(per // 2):
-        half, m, t = pair_place(step * (per // 2) + k, mir_ref.shape[1])
-        a, b = mir_ref[half, m, 0, t].astype(F32), mir_ref[half, m, 1, t].astype(F32)
+    per = cols // STEPS
+
+    def mixed(n, carry):
+        half, m, t = pair_place(n, mir.shape[1])
+        a, b = mir[half, m, 0, t].astype(F32), mir[half, m, 1, t].astype(F32)
         even = jnp.where(low, a, pltpu.roll(b, lanes // 2, 1))
         odd = jnp.where(low, pltpu.roll(a, lanes // 2, 1), b)
-        log_ref[2 * k] = (hl_ref[2 * k].astype(F32) + even).astype(BF16)
-        log_ref[2 * k + 1] = (hl_ref[2 * k + 1].astype(F32) + odd).astype(BF16)
-
-    @pl.when(step == 0)
-    def _():
-        width = sum_ref.shape[1]
-        for k in range(hidden // width):
-            span = slice(k * width, (k + 1) * width)
-            gg_ref[:, span] = sum_ref[k * width:(k + 1) * width, :].astype(F32)
-            gu_ref[:, span] = sum_ref[hidden + k * width:hidden + (k + 1) * width, :].astype(F32)
-        go_ref[...] = sum_ref[2 * hidden:3 * hidden, :].astype(F32)
-        at = 3 * hidden
-        gd_ref[...] = sum_ref[at:at + gd_ref.shape[0], :].astype(F32)
-        at += gd_ref.shape[0]
-        gt_ref[...] = sum_ref[at:at + gt_ref.shape[0], :].astype(F32)
-        at += gt_ref.shape[0]
-        norm = sum_ref[at:at + 16, :].astype(F32)
-        gn_ref[0:1, :] = jnp.sum(norm[0:8], axis=0, keepdims=True)
-        gn_ref[1:2, :] = jnp.sum(norm[8:16], axis=0, keepdims=True)
-
-
-def finish(hidden, slot_of, count, back, mir, hl, sums, grad_pair):
+        local[2 * n] = (local[2 * n].astype(F32) + even).astype(BF16)
+        local[2 * n + 1] = (local[2 * n + 1].astype(F32) + odd).astype(BF16)
+        return carry
+
+    for i in range(STEPS):
+        if i:
+            pair_in[i].wait()
+            leaving.append(begin(gp.at[bands[i]], out_ref.at[bands[i]], gp_out.at[i]))
+        lax.fori_loop(i * per // 2, (i + 1) * per // 2, mixed, 0, unroll=2)
+        part = pl.ds(i * per, per)
+        leaving.append(begin(local.at[part], log_ref.at[part], log_sem.at[i]))
+    for copy in leaving:
+        copy.wait()
+
+
+def finish(hidden, slot_of, back, mir, hl, sums, grad_pair):
     slots = slot_of.shape[0]
-    feature, cells = back.shape[2], back.shape[0] * back.shape[3]
+    chunks, _, feature, span = back.shape
     cols, bins, rows = hl.shape
     width = sums.shape[1]
-    per, each = cols // STEPS, slots // STEPS
-    const = lambda shape: pl.BlockSpec(shape, lambda i, s: (0,) * len(shape))
-    outs = [((slots, feature, cells), BF16), ((cols, bins, rows), BF16), (grad_pair.shape, F32),
+    outs = [((slots, feature, chunks * span), BF16), (hl.shape, BF16), (grad_pair.shape, F32),
             ((feature, width), F32), ((width, hidden), F32), ((width, hidden), F32), ((hidden, width), F32),
-            ((bins, width), F32), ((2, width), F32)]
-    held = lambda n: pl.BlockSpec(
-        (back.shape[0], 1, feature, back.shape[3]), lambda i, s: (0, s[i * each + n], 0, 0))
-    band = pl.BlockSpec((grad_pair.shape[0] // STEPS,) + grad_pair.shape[1:], lambda i, s: (i, 0, 0))
+            ((bins, width), F32), ((1, width), F32), ((1, width), F32)]
+    dma = lambda n: pltpu.SemaphoreType.DMA((n,))
     return pl.pallas_call(
         functools.partial(finish_kernel, hidden),
         name="finish",
-        grid_spec=pltpu.PrefetchScalarGridSpec(
-            num_scalar_prefetch=1,
-            grid=(STEPS,),
-            in_specs=[held(n) for n in range(each)] + [
-                pl.BlockSpec(memory_space=pltpu.SMEM),
-                const(mir.shape),
-                pl.BlockSpec((per, bins, rows), lambda i, s: (i, 0, 0)),
-                const(sums.shape),
-                band,
-            ],
-            out_specs=[
-                pl.BlockSpec((each, feature, cells), lambda i, s: (i, 0, 0)),
-                pl.BlockSpec((per, bins, rows), lambda i, s: (i, 0, 0)),
-                band,
-            ] + [const(shape) for shape, _ in outs[3:]],
-        ),
+        in_specs=[smem()] + [hbm()] * 5,
+        out_specs=[hbm()] * 3 + [vmem()] * 7,
         out_shape=[jax.ShapeDtypeStruct(shape, kind) for shape, kind in outs],
-        compiler_params=pltpu.CompilerParams(
-            dimension_semantics=("arbitrary",), vmem_limit_bytes=VMEM_LIMIT),
-    )(slot_of, *([back] * each), count, mir, hl, sums, grad_pair)
+        scratch_shapes=[
+            pltpu.VMEM(mir.shape, BF16),
+            pltpu.VMEM(hl.shape, BF16),
+            pltpu.VMEM(sums.shape, BF16),
+            pltpu.VMEM(grad_pair.shape, F32),
+            pltpu.VMEM((slots, feature, chunks * span), BF16),
+            pltpu.SemaphoreType.DMA((slots, chunks)), dma(3), dma(STEPS), dma(STEPS), dma(slots), dma(STEPS),
+        ],
+        compiler_params=pltpu.CompilerParams(vmem_limit_bytes=14 * 1024 * 1024),
+    )(slot_of, back, mir, hl, sums, grad_pair)
 
 
 def per_device(pair, logit_cotangent, tiles, tile_target, tile_square, tile_count, w_template,
@@ -673,16 +694,16 @@
     back, mir_heads, sums, gp, hl, _ = window(
         row_devs, col_devs, 1.0 / length, code, tiles_t, cot_t, pair, w_template,
         transition_norm_gain[None, :], transition_norm_bias[None, :], w_gate, w_up, w_out, w_dist.T)
-    grad_tiles_t, logits_t, grad_pair, g_template, g_gate, g_up, g_out, g_dist_t, g_norm = finish(
-        hidden, slot_of, tile_count, back.reshape(CHUNKS, col_devs * CAP, feature, SPAN), mir_heads, hl,
+    grad_tiles_t, logits_t, grad_pair, g_template, g_gate, g_up, g_out, g_dist_t, g_gain, g_bias = finish(
+        hidden, slot_of, back.reshape(CHUNKS, col_devs * CAP, feature, SPAN), mir_heads, hl,
         sums.reshape(ROWS_SUM, width), gp)
     return (
         jnp.transpose(logits_t, (2, 0, 1)),
         grad_pair,
         jnp.transpose(grad_tiles_t, (0, 2, 1)),
         g_template,
-        g_norm[0],
-        g_norm[1],
+        g_gain.reshape(width),
+        g_bias.reshape(width),
         g_gate,
         g_up,
         g_out,

time: 152 us -> 160 us (1.053)
  local copies, waits for them, and re-layouts: 1.91 us -> 10.5 us
    unnamed x2 -> x20, local copies, waits for them, and re-layouts: 0.01 us -> 10.5 us
    pallas_call x1, Pallas kernels: 8.48 us -> 6.26 us  [finish(): pl.pallas_call(functools.partial(finish_kernel, hidden), name='finish', i...]
    pallas_call x1, Pallas kernels: 137 us -> 138 us  [window(): pl.pallas_call(functools.partial(window_kernel, row_devs, col_devs, scale...]
where the time goes in v6:
time: 160 us; the launch traced here: 157 us
  Pallas kernels  144 us (90%)
  local copies, waits for them, and re-layouts  10.5 us (7%)
  other arithmetic  1.7 us (1%)
    pallas_call x1, Pallas kernels, window(): pl.pallas_call(functools.partial(window_kernel, row_devs, col_devs, scale...  138 us
    unnamed x20, local copies, waits for them, and re-layouts  10.5 us
    pallas_call x1, Pallas kernels, finish(): pl.pallas_call(functools.partial(finish_kernel, hidden), name='finish', i...  6.26 us

profile of v6, /device:TPU:1, one launch (start us, length us, event | category | flops | bytes accessed | tf_op | source)
XLA Modules:
  0.0 157.5 jit_solution(3172554786233366068)
XLA Ops:
  0.6 0.9 convert_reduce_fusion
  1.6 0.7 multiply_add_fusion
  2.3 0.1 select_reduce_fusion
  2.3 0.1 reshape.45.code_ref
  2.4 0.0 copy-start.1
  2.4 1.6 %copy-done.1 = bf16[16,1024,64]{1,2,0:T(8,128)(2,1)S(1)} copy-done((bf16[16,1024,64]{1,2,0:T(8,128)(2,1)S(1)}, bf16[16,1024,64]{1,2,0:T(8,128)(2,1)}, u32[]{:S(2)}) %copy-start.1) | copy-done | bytes 2097176
  4.0 0.0 copy-start.2
  4.0 1.2 copy-done.2
  5.3 0.0 copy-start.3
  5.3 0.9 copy-done.3
  6.2 0.0 copy-start.4
  6.2 0.9 copy-done.4
  7.1 0.0 copy-start.5
  7.1 0.9 copy-done.5
  8.0 0.0 copy-start.6
  8.0 0.7 copy-done.6
  8.7 0.0 copy-start.7
  8.7 0.7 copy-done.7
  9.4 0.7 copy-done.8
  10.1 0.7 copy-done.9
  10.7 138.1 %window.1 = (bf16[4,16,2,64,256]{4,3,2,1,0:T(8,128)(2,1)S(1)}, bf16[2,4,2,4,64,128]{5,4,3,2,1,0:T(8,128)(2,1)S(1)}, bf16[8,16,16,128]{3,2,1,0:T(8,128)(2,1)S(1)}...) custom-call(s32[16,2]{1,0:T(8,128)S(1)} %reshape.45.code_ref, ...), custom_call_target="tpu_custom_call" | custom-call | tf_op jit(solution)/shard_map/window/pallas_call | solution.py:519
  148.8 0.0 copy-start
  148.9 2.2 %copy-done = f32[128,64,128]{2,1,0:T(8,128)S(1)} copy-done((f32[128,64,128]{2,1,0:T(8,128)S(1)}, f32[128,64,128]{2,1,0:T(8,128)}, u32[]{:S(2)}) %copy-start) | copy-done | bytes 4194328
  151.0 6.3 %finish.1 = (bf16[16,64,1024]{2,1,0:T(8,128)(2,1)}, bf16[64,64,128]{2,1,0:T(8,128)(2,1)}, f32[128,64,128]{2,1,0:T(8,128)}, f32[64,128]{1,0:T(8,128)}, f32[128,51...) custom-call(s32[16]{0:T(128)S(1)} %get-tuple-element.41.slot_ref, ...), custom_call_target="tpu_custom_call" | custom-call | tf_op jit(solution)/shard_map/finish/pallas_call | solution.py:657
  (2 shorter events, 0.0 us)
Async XLA Ops:
  2.4 1.6 %copy-start.1 = (bf16[16,1024,64]{1,2,0:T(8,128)(2,1)S(1)}, bf16[16,1024,64]{1,2,0:T(8,128)(2,1)}, u32[]{:S(2)}) copy-start(bf16[16,1024,64]{1,2,0:T(8,128)(2,1)} %param.15) | copy-start | bytes 6291460
  4.0 1.2 copy-start.2
  5.3 0.9 copy-start.3
  6.2 0.9 copy-start.4
  7.1 0.9 copy-start.5
  8.0 0.7 copy-start.6
  8.7 0.7 copy-start.7
  9.4 0.7 copy-start.8
  10.1 0.7 copy-start.9
  148.8 2.2 %copy-start = (f32[128,64,128]{2,1,0:T(8,128)S(1)}, f32[128,64,128]{2,1,0:T(8,128)}, u32[]{:S(2)}) copy-start(f32[128,64,128]{2,1,0:T(8,128)} %get-tuple-element.29.gp_ref) | copy-start | bytes 12582916

commit v7 on v5

--- a/solution.py
+++ b/solution.py
@@ -174,6 +174,7 @@
 CHUNKS = SQ // BAND
 SPAN = BAND * SQ
 PART = 256
+EARLY, MIDDLE = 7, 5
 
 
 def share(count):
@@ -408,8 +409,8 @@
         back_copies.append(to_all(lambda to: sendbuf.at[q, to], lambda n: back_ref.at[q, col],
                                   lambda n: g_send.at[q, n], lambda n: g_recv.at[q, n]))
         own_back.append(local(sendbuf.at[q, col], back_ref.at[q, col], own_g.at[q]))
-        if q < CHUNKS - 2:
-            for copy in back_copies[q]:
+        if q < CHUNKS - 1:
+            for copy in back_copies[q] if q < CHUNKS - 2 else back_copies[q][:EARLY]:
                 copy.start()
 
     for k in range(hidden // width):
@@ -439,8 +440,7 @@
             recv_sem=a_recv.at[k - 1], device_id=(to, col), device_id_type=MESH))
     for copy in first:
         copy.start()
-    held = back_copies[2] + back_copies[3]
-    some = len(order) // 3
+    held = back_copies[2][EARLY:] + back_copies[3]
 
     wd = wd_ref[...]
 
@@ -462,7 +462,7 @@
                     lambda n: b_send.at[n], lambda n: b_recv.at[n])
     for copy in second:
         copy.start()
-    for copy in held[:some]:
+    for copy in held[:MIDDLE]:
         copy.start()
     halves[0].finish_2()
     halves[0].start_3()
@@ -476,7 +476,7 @@
     gather = to_all(lambda to: piece, lambda n: chunk.at[col], lambda n: e_send.at[n], lambda n: e_recv.at[n])
     for copy in gather:
         copy.start()
-    for copy in held[some:]:
+    for copy in held[MIDDLE:]:
         copy.start()
     halves[1].finish_2()
     halves[1].start_3()
@@ -570,14 +570,14 @@
     )(code, tiles_t, cot_t, pair, *weights)
 
 
-STEPS = 4
+STEPS = 2
 
 
 def finish_kernel(hidden, slot_ref, *refs):
     each = slot_ref.shape[0] // STEPS
     backs, refs = refs[:each], refs[each:]
     (count_ref, mir_ref, hl_ref, sum_ref, gp_ref,
-     tile_ref, log_ref, out_ref, gt_ref, gg_ref, gu_ref, go_ref, gd_ref, gn_ref) = refs
+     tile_ref, log_ref, out_ref, gt_ref, gg_ref, gu_ref, go_ref, gd_ref, gn_ref, gb_ref) = refs
     step = pl.program_id(0)
     out_ref[...] = gp_ref[...]
     for n, back_ref in enumerate(backs):
@@ -609,8 +609,8 @@
         gt_ref[...] = sum_ref[at:at + gt_ref.shape[0], :].astype(F32)
         at += gt_ref.shape[0]
         norm = sum_ref[at:at + 16, :].astype(F32)
-        gn_ref[0:1, :] = jnp.sum(norm[0:8], axis=0, keepdims=True)
-        gn_ref[1:2, :] = jnp.sum(norm[8:16], axis=0, keepdims=True)
+        gn_ref[...] = jnp.sum(norm[0:8], axis=0, keepdims=True)
+        gb_ref[...] = jnp.sum(norm[8:16], axis=0, keepdims=True)
 
 
 def finish(hidden, slot_of, count, back, mir, hl, sums, grad_pair):
@@ -622,7 +622,7 @@
     const = lambda shape: pl.BlockSpec(shape, lambda i, s: (0,) * len(shape))
     outs = [((slots, feature, cells), BF16), ((cols, bins, rows), BF16), (grad_pair.shape, F32),
             ((feature, width), F32), ((width, hidden), F32), ((width, hidden), F32), ((hidden, width), F32),
-            ((bins, width), F32), ((2, width), F32)]
+            ((bins, width), F32), ((1, width), F32), ((1, width), F32)]
     held = lambda n: pl.BlockSpec(
         (back.shape[0], 1, feature, back.shape[3]), lambda i, s: (0, s[i * each + n], 0, 0))
     band = pl.BlockSpec((grad_pair.shape[0] // STEPS,) + grad_pair.shape[1:], lambda i, s: (i, 0, 0))
@@ -673,7 +673,7 @@
     back, mir_heads, sums, gp, hl, _ = window(
         row_devs, col_devs, 1.0 / length, code, tiles_t, cot_t, pair, w_template,
         transition_norm_gain[None, :], transition_norm_bias[None, :], w_gate, w_up, w_out, w_dist.T)
-    grad_tiles_t, logits_t, grad_pair, g_template, g_gate, g_up, g_out, g_dist_t, g_norm = finish(
+    grad_tiles_t, logits_t, grad_pair, g_template, g_gate, g_up, g_out, g_dist_t, g_gain, g_bias = finish(
         hidden, slot_of, tile_count, back.reshape(CHUNKS, col_devs * CAP, feature, SPAN), mir_heads, hl,
         sums.reshape(ROWS_SUM, width), gp)
     return (
@@ -681,8 +681,8 @@
         grad_pair,
         jnp.transpose(grad_tiles_t, (0, 2, 1)),
         g_template,
-        g_norm[0],
-        g_norm[1],
+        g_gain.reshape(width),
+        g_bias.reshape(width),
         g_gate,
         g_up,
         g_out,

time: 152 us -> 153 us (level)
  the two profiles are of different devices: /device:TPU:1 before, /device:TPU:16 now
where the time goes in v7:
time: 153 us
  Pallas kernels  150 us (98%)
  other arithmetic  1.7 us (1%)
    pallas_call x1, Pallas kernels, window(): pl.pallas_call(functools.partial(window_kernel, row_devs, col_devs, scale...  142 us
    pallas_call x1, Pallas kernels, finish(): pl.pallas_call(functools.partial(finish_kernel, hidden), name='finish', g...  7.36 us

profile of v7, /device:TPU:16, one launch (start us, length us, event | category | flops | bytes accessed | tf_op | source)
XLA Modules:
  0.0 153.0 jit_solution(2674447137761548943)
XLA Ops:
  0.6 0.9 convert_reduce_fusion
  1.6 0.7 multiply_add_fusion
  2.3 0.0 copy-start
  2.3 0.1 select_reduce_fusion
  2.3 0.7 reshape.45.code_ref
  3.0 142.4 %window.1 = (bf16[4,16,2,64,256]{4,3,2,1,0:T(8,128)(2,1)}, bf16[2,4,2,4,64,128]{5,4,3,2,1,0:T(8,128)(2,1)}, bf16[8,16,16,128]{3,2,1,0:T(8,128)(2,1)}, f32[128,64...) custom-call(s32[16,2]{1,0:T(8,128)} %reshape.45.code_ref, bf16[16,64,1024]{2,1,0:T(8,128)(2,1)} %bitcast.22, ...), custom_call_target="tpu_custom_call" | custom-call | tf_op jit(solution)/shard_map/window/pallas_call | solution.py:518
  145.4 0.0 copy-done
  145.5 7.4 %finish.1 = (bf16[16,64,1024]{2,1,0:T(8,128)(2,1)}, bf16[64,64,128]{2,1,0:T(8,128)(2,1)}, f32[128,64,128]{2,1,0:T(8,128)}, f32[64,128]{1,0:T(8,128)}, f32[128,51...) custom-call(s32[16]{0:T(128)} %copy-done, ...), custom_call_target="tpu_custom_call" | custom-call | tf_op jit(solution)/shard_map/finish/pallas_call | solution.py:629
Async XLA Ops:
  2.3 143.2 %copy-start = (s32[16]{0:T(128)}, s32[16]{0:T(128)S(1)}, u32[]{:S(2)}) copy-start(s32[16]{0:T(128)S(1)} %get-tuple-element.41.slot_ref) | copy-start | bytes 196
